TPU v7x, 128 devices: a whole 4x4x4 slice. The times are simulated.
128 devices in a mesh: row: 8 (over x, z_hi), col: 16 (over z_lo, y, core).
Axes of the slice: x: 4, y: 4, z: 4 (z_hi: 2, z_lo: 2; z = z_hi * 2 + z_lo), core: 2. Of those that a mesh axis runs over, the one named last changes fastest.
Arguments:
- coeffs: bfloat16 [128, 512, 128], P(('row', 'col')), may hold values from -6 to 6
- trial: bfloat16 [128, 32, 128], P(('row', 'col')), may hold values from -6 to 6
- screened: bfloat16 [128, 512, 512], P('col'), may hold values from -9.1552734e-05 to 9.1552734e-05
- qmap: int32 [128, 128], replicated, may hold values from 0 to 127, as said below
- mask: int32 [128, 128], replicated, may hold values from 0 to 1, as said below
Outputs:
- product: float32 [128, 32, 128], P(('row', 'col'))
Inputs may be any that keep to these rules, and one draw needn't show every extreme that they name: qmap[k, k'] depends on k - k' modulo 128 only. Over the pairs (k, k') of one tile of 16 rows by 8 columns at offsets that are multiples of 16 and 8, at most 2 distinct values fall in any group q // 8; the same holds for the pairs (k', k); some tile reaches 2. mask[k, k] = 1 and mask[k, k'] + mask[k', k] = 1 for k != k'.
All inputs are finite; a program needn't handle non-finite values.
Results may differ from a plain program's by a relative error of at most 0.004.
Values may be sent and summed in bfloat16 or wider, within the bound.
A program may use at most 192 MiB of HBM per device.

v0:
```python
import jax
import jax.numpy as jnp
from jax import lax
from jax.sharding import PartitionSpec as P


def in_one_piece(arrays, axis, dim, along):
    widths = [a.shape[along] for a in arrays]
    both = jnp.concatenate(arrays, axis=along)
    whole = lax.all_gather(both, axis, axis=dim, tiled=True)
    return tuple(jnp.split(whole, [sum(widths[:k]) for k in range(1, len(widths))], axis=along))


def from_root(shard, axis, root):
    return lax.dynamic_index_in_dim(lax.all_gather(shard, axis), root, 0, keepdims=False)


def in_blocks(shard, dim, devices):
    dims = shard.shape
    tiles = shard.reshape(*dims[:dim], devices, dims[dim] // devices, *dims[dim + 1 :])
    return jnp.moveaxis(tiles, dim, 0)


def sent_and_summed(shard, axis, dim):
    devices = lax.axis_size(axis)
    tiles = lax.all_to_all(in_blocks(shard, dim, devices), axis, 0, 0, tiled=True)
    return jnp.sum(tiles, axis=0)


def pack_slots(screened, wanted_all, col_pos, capacity):
    per_owner = screened.shape[0]
    owned_q = col_pos * per_owner + jnp.arange(per_owner, dtype=jnp.int32)
    needed = jnp.any(wanted_all[:, :, None] == owned_q[None, None, :], axis=1).astype(jnp.int32)
    ranking = jnp.cumsum(needed, axis=1) - 1
    matches = (needed[:, None, :] == 1) & (
        ranking[:, None, :] == jnp.arange(capacity, dtype=jnp.int32)[None, :, None]
    )
    source = jnp.sum(
        jnp.where(matches, jnp.arange(per_owner, dtype=jnp.int32)[None, None, :], 0), axis=2
    )
    parcel = jnp.take(screened, source.reshape(-1), axis=0)
    return parcel.reshape(wanted_all.shape[0], capacity, screened.shape[1], screened.shape[2])


def slot_table(wanted_own, n_col, per_owner, capacity):
    count_q = n_col * per_owner
    present = jnp.any(wanted_own[:, None] == jnp.arange(count_q, dtype=jnp.int32)[None, :], axis=0)
    ranking = jnp.cumsum(present.reshape(n_col, per_owner).astype(jnp.int32), axis=1) - 1
    return (jnp.arange(n_col, dtype=jnp.int32)[:, None] * capacity + ranking).reshape(count_q)


def locate(values, table):
    hits = values[..., None] == jnp.arange(table.shape[0], dtype=jnp.int32)
    return jnp.sum(jnp.where(hits, table, 0), axis=-1)


def per_device(coeffs, trial, screened, qmap, mask):
    n_col = lax.axis_size("col")
    row_pos = lax.axis_index("row")
    col_pos = lax.axis_index("col")
    row_coeffs, row_trial = in_one_piece((coeffs, trial), "col", 0, 1)
    k_row = row_coeffs.shape[0]
    k_col = k_row // 2
    half_start = col_pos % 2 * k_col
    own_coeffs = lax.dynamic_slice_in_dim(row_coeffs, half_start, k_col, 0)
    own_trial = lax.dynamic_slice_in_dim(row_trial, half_start, k_col, 0)
    col_coeffs, col_trial = (
        from_root(own_coeffs, "row", col_pos // 2),
        from_root(own_trial, "row", col_pos // 2),
    )
    per_owner = screened.shape[0]
    row_start = row_pos * k_row
    col_start = col_pos * k_col
    row_q = lax.dynamic_slice_in_dim(qmap, row_start, k_row, 0)
    tile_q = lax.dynamic_slice_in_dim(row_q, col_start, k_col, 1)
    row_mask = lax.dynamic_slice_in_dim(mask, row_start, k_row, 0)
    tile_mask = lax.dynamic_slice_in_dim(row_mask, col_start, k_col, 1).astype(jnp.float32)
    wanted_all = jnp.transpose(row_q.reshape(k_row, n_col, k_col), (1, 0, 2)).reshape(
        n_col, k_row * k_col
    )
    wanted_own = tile_q.reshape(-1)
    single = (k_row + k_col - 2) // n_col + 1
    col_q = lax.dynamic_slice_in_dim(qmap, row_start, k_row, 1)
    mirror_q = jnp.transpose(lax.dynamic_slice_in_dim(col_q, col_start, k_col, 0))
    wanted_all = jnp.concatenate([wanted_all, col_q.reshape(n_col, k_col * k_row)], axis=1)
    wanted_own = jnp.concatenate([wanted_own, mirror_q.reshape(-1)])
    capacity = 2 * single
    parcel = pack_slots(screened, wanted_all, col_pos, capacity)
    received = lax.all_to_all(parcel, "col", split_axis=0, concat_axis=0, tiled=True)
    received = received.reshape(n_col * capacity, screened.shape[1], screened.shape[2])
    table = slot_table(wanted_own, n_col, per_owner, capacity)
    tile_slots = locate(tile_q, table)
    mirror_slots = locate(mirror_q, table)

    def sweep(carry, inputs):
        coeff_row, slot_row, mirror_row, mask_row = inputs
        direct = mask_row > 0.5
        slots = jnp.where(direct, slot_row, mirror_row)
        picked = jnp.take(received, slots, axis=0)
        left_side = jnp.where(direct[:, None, None], coeff_row[None], col_coeffs)
        right_side = jnp.where(direct[:, None, None], col_coeffs, coeff_row[None])
        halves = jnp.einsum(
            "jrt,jrs->jts", left_side, picked, preferred_element_type=jnp.float32
        ).astype(jnp.bfloat16)
        blocks = jnp.einsum(
            "jts,jsu->jtu", halves, right_side, preferred_element_type=jnp.float32
        ).astype(jnp.bfloat16)
        kernel_row = jnp.where(direct[:, None, None], blocks, jnp.transpose(blocks, (0, 2, 1)))
        forward = jnp.einsum(
            "jtu,jvu->vt", kernel_row, col_trial, preferred_element_type=jnp.float32
        )
        return (carry, forward)

    _, rows_out = lax.scan(
        sweep, jnp.float32(0.0), (row_coeffs, tile_slots, mirror_slots, tile_mask)
    )
    return sent_and_summed(rows_out, "col", 0)


def solution(mesh):
    return jax.shard_map(
        per_device,
        mesh=mesh,
        in_specs=(
            P(("row", "col"), None, None),
            P(("row", "col"), None, None),
            P("col", None, None),
            P(),
            P(),
        ),
        out_specs=P(("row", "col"), None, None),
        check_vma=False,
    )
```

profile of v0, /device:TPU:0, one launch (start us, length us, event | category | flops | bytes accessed | tf_op | source)
XLA Modules:
  0.0 705.6 jit_solution(13316041538290301818)
XLA Ops:
  6.5 0.7 constant_dynamic-slice_fusion.5
  7.2 0.9 constant_dynamic-slice_fusion.4
  9.6 14.3 %gather_fusion.1 = bf16[64,512,512]{2,1,0:T(8,128)(2,1)} fusion(bf16[8,512,512]{2,1,0:T(8,128)(2,1)} %param.9, s32[1024]{0:T(1024)S(1)} %pad_clamp_fusion.1), kind=kCustom, calls=%fused_computation.1 | custom fusion | bytes 67109120 | tf_op jit(solution)/shard_map/jit(_take)/gather | solution.py:41
  24.0 22.8 %broadcast_select_fusion = bf16[16,4,512,512]{3,2,1,0:T(8,128)(2,1)} fusion(bf16[16,4,512,512]{3,2,1,0:T(8,128)(2,1)} %bitcast.70, pred[16,4]{1,0:T(8,128)(4,1)S(1)} %copy.32), kind=kLoop, calls=%fused_computation.31 | loop fusion | flops 16777216 | bytes 67108928 | tf_op jit(solution)/shard_map/jit(_take)/select_n | solution.py:41
  46.8 6.2 all-to-all-start
  53.9 203.7 %all-gather.5.cloned.1.call-done = bf16[16,544,128]{2,1,0:T(8,128)(2,1)} async-done(((bf16[1,544,128]{2,1,0:T(8,128)(2,1)}), bf16[16,544,128]{2,1,0:T(8,128)(2,1)}) %all-gather.5.cloned.1.call-update) | async-done | bytes 2228240 | tf_op jit(solution)/shard_map/all_gather | solution.py:10
  257.6 1.8 split.8
  259.4 1.1 constant_dynamic-slice_fusion.6
  260.5 0.8 dynamic_slice.48
  261.3 0.8 dynamic-slice_bitcast_fusion.3
  262.9 0.8 dynamic-slice_convert_fusion
  264.4 204.8 %all-gather.1 = bf16[64,32,128]{2,1,0:T(8,128)(2,1)S(1)} all-gather(bf16[8,32,128]{2,1,0:T(8,128)(2,1)S(1)} %constant_dynamic-slice_fusion.3), channel_id=3, replica_groups=mesh['row'=8,'col'=16] {'row'}, dimensions={0}, use_global_device_ids=true | all-gather | bytes 589824 | tf_op jit(solution)/shard_map/all_gather | solution.py:15
  469.2 49.5 %all-gather.7.cloned.1.call-done = bf16[64,512,128]{2,1,0:T(8,128)(2,1)} async-done(((bf16[8,512,128]{2,1,0:T(8,128)(2,1)}), bf16[64,512,128]{2,1,0:T(8,128)(2,1)}) %all-gather.7.cloned.1.call-update) | async-done | bytes 8388624 | tf_op jit(solution)/shard_map/all_gather | solution.py:15
  518.7 2.3 dynamic-slice_bitcast_fusion.1
  521.1 154.5 %while.10 = (s32[]{:T(128)}, f32[16,32,128]{2,1,0:T(8,128)S(1)}, f32[16,8]{1,0:T(8,128)S(1)}, bf16[16,512,128]{2,1,0:T(8,128)(2,1)S(1)}, bf16[8,512,128]{2,1,0:T...) while((s32[]{:T(128)}, f32[16,32,128]{2,1,0:T(8,128)S(1)}, ...), condition=%wide.region_8.9_spmd, body=%wide.region_7.8_spmd.sunk | while | flops 683410560 | bytes 15422425 | solution.py:114
  521.1 5.0 gather_fusion
  526.2 4.1 fusion.42
  530.8 5.0 gather_fusion
  535.8 4.1 fusion.42
  540.4 5.0 gather_fusion
  545.5 4.1 fusion.42
  550.1 5.0 gather_fusion
  555.1 4.1 fusion.42
  559.7 5.0 gather_fusion
  564.8 4.1 fusion.42
  569.4 5.0 gather_fusion
  574.5 4.1 fusion.42
  579.0 5.0 gather_fusion
  584.1 4.1 fusion.42
  588.7 5.0 gather_fusion
  593.8 4.1 fusion.42
  598.3 5.0 gather_fusion
  603.4 4.1 fusion.42
  608.0 5.0 gather_fusion
  613.1 4.1 fusion.42
  617.7 5.0 gather_fusion
  622.7 4.1 fusion.42
  627.3 5.0 gather_fusion
  632.4 4.1 fusion.42
  637.0 5.0 gather_fusion
  642.0 4.1 fusion.42
  646.6 5.0 gather_fusion
  651.7 4.1 fusion.42
  656.3 5.0 gather_fusion
  661.3 4.1 fusion.42
  665.9 5.0 gather_fusion
  671.0 4.1 fusion.42
  675.6 22.6 %all_to_all.10 = f32[16,1,32,128]{3,2,1,0:T(8,128)S(1)} all-to-all(f32[16,1,32,128]{3,2,1,0:T(8,128)S(1)} %bitcast.72), channel_id=1, replica_groups=mesh['row'=8,'col'=16] {'col'}, dimensions={0} | all-to-all | bytes 524288 | tf_op jit(solution)/shard_map/all_to_all | solution.py:26
  (159 shorter events, 12.5 us)
Async XLA Ops:
  46.8 6.3 copy-start
  46.8 6.3 copy-start.1
  46.8 474.3 %all-to-all-start = ((bf16[16,4,512,512]{3,2,1,0:T(8,128)(2,1)}), bf16[16,4,512,512]{3,2,1,0:T(8,128)(2,1)}, u32[]{:S(2)}, u32[]{:S(2)}) async-start(bf16[16,4,512,512]{3,2,1,0:T(8,128)(2,1)} %broadcast_select_fusion), calls=%async_computation | async-start | bytes 67108864 | tf_op jit(solution)/shard_map/all_to_all | solution.py:89
  53.0 204.5 %all-gather.5.cloned.1.call-start = ((), (), s32[]{:S(2)}) async-start(), calls=%async_computation.2 | async-start | bytes 2367488 | tf_op jit(solution)/shard_map/all_gather | solution.py:10
  53.8 464.9 %all-gather.7.cloned.1.call-start = ((), (), s32[]{:S(2)}) async-start(), calls=%async_computation.3 | async-start | bytes 9437184 | tf_op jit(solution)/shard_map/all_gather | solution.py:15
  257.6 6.8 slice-start
Sparse Core Ops, SparseCore 0:
  55.6 201.9 all-gather.4
  260.6 258.0 all-gather.6
where the time goes:
time: 707 us; the launch traced here: 706 us
  waiting for transfers between devices  253 us (36%)
  blocking collectives  227 us (32%)
  local copies, waits for them, and re-layouts  107 us (15%)
  matrix products  69.6 us (10%)
  other arithmetic  27.6 us (4%)
  between operations  13.6 us (2%)
    all_gather x1, blocking collectives, from_root(): lax.all_gather(shard, axis)  205 us
    all_gather x1, waiting for transfers between devices, in_one_piece(): whole = lax.all_gather(both, axis, axis=dim, tiled=True)  204 us
    gather x16, local copies, waits for them, and re-layouts, sweep(): picked = jnp.take(received, slots, axis=0)  80.1 us
    dot_general x16, matrix products, sweep(): jnp.einsum('jts,jsu->jtu', halves, right_side, preferred_element_type=jnp...  65.5 us
    all_gather x1, waiting for transfers between devices, from_root(): lax.all_gather(shard, axis)  49.5 us
    select_n x2, other arithmetic, pack_slots(): parcel = jnp.take(screened, source.reshape(-1), axis=0)  22.8 us
    all_to_all x1, blocking collectives, sent_and_summed(): lax.all_to_all(in_blocks(shard, dim, devices), axis, 0, 0, tiled=True)  22.6 us
    gather x1, local copies, waits for them, and re-layouts, pack_slots(): parcel = jnp.take(screened, source.reshape(-1), axis=0)  14.3 us
  transfers between devices with their start and end apart: 3, of which 2 were waited for; matrix products, arithmetic and copies ran while one was open for 1% of the time, Pallas kernels for 0%

commit v1 on v0

v1 whole, which is shorter than its diff:
```python
import jax
import jax.numpy as jnp
from jax import lax
from jax.experimental import pallas as pl
from jax.experimental.pallas import tpu as pltpu
from jax.sharding import PartitionSpec as P


def apply_kernel(n_row_k, per_owner, qrow_hbm, mask_hbm, vecs_hbm, w_hbm, out_ref,
                 vecs, wbuf, qrow, masks, found, sems, wsems):
    total = vecs_hbm.shape[0]
    nv = vecs_hbm.shape[1]
    row_pos = lax.axis_index("row")
    col_pos = lax.axis_index("col")
    k0 = row_pos * n_row_k
    copies = [
        pltpu.make_async_copy(qrow_hbm.at[pl.ds(0, 1)], qrow, sems.at[0]),
        pltpu.make_async_copy(mask_hbm.at[pl.ds(k0, n_row_k)], masks, sems.at[1]),
        pltpu.make_async_copy(vecs_hbm, vecs.at[pl.ds(0, total)], sems.at[2]),
        pltpu.make_async_copy(vecs_hbm.at[pl.ds(0, n_row_k)], vecs.at[pl.ds(total, n_row_k)], sems.at[3]),
    ]
    for copy in copies:
        copy.start()
    wcopies = [pltpu.make_async_copy(w_hbm.at[j], wbuf.at[j], wsems.at[j]) for j in range(per_owner)]
    for copy in wcopies:
        copy.start()
    out_ref[...] = jnp.zeros_like(out_ref)
    copies[0].wait()
    copies[1].wait()

    def scan(d, count):
        q = qrow[0, lax.rem(total - d, total)]
        found[count] = d
        return count + (q // per_owner == col_pos).astype(jnp.int32)

    count = lax.fori_loop(0, total, scan, jnp.int32(0))
    copies[2].wait()
    copies[3].wait()
    for copy in wcopies:
        copy.wait()

    def side(start, weights):
        blocks = []
        for i in range(n_row_k):
            scale = jnp.full((nv, vecs.shape[2]), weights[i], jnp.float32).astype(jnp.bfloat16)
            blocks.append(vecs[start + i] * scale)
        return jnp.concatenate(blocks, axis=0)

    def step(j, carry):
        d = found[j]
        q = qrow[0, lax.rem(total - d, total)]
        w = wbuf[q - col_pos * per_owner]
        ahead, behind = [], []
        for i in range(n_row_k):
            ahead.append(masks[i, lax.rem(k0 + i + total - d, total)].astype(jnp.float32))
            mirror = 1 - masks[i, lax.rem(k0 + i + d, total)]
            behind.append(jnp.where(d == 0, 0, mirror).astype(jnp.float32))
        direct = side(lax.rem(k0 + total - d, total), ahead)
        out_ref[...] += lax.dot_general(
            direct, w, (((1,), (1,)), ((), ())), preferred_element_type=jnp.float32
        )
        turned = side(lax.rem(k0 + d, total), behind)
        out_ref[...] += jnp.dot(turned, w, preferred_element_type=jnp.float32)
        return carry

    lax.fori_loop(0, count, step, 0)


def apply(qmap, mask, vecs, screened, n_row_k):
    total, nv, rank = vecs.shape
    per_owner = screened.shape[0]
    return pl.pallas_call(
        lambda *refs: apply_kernel(n_row_k, per_owner, *refs),
        out_shape=jax.ShapeDtypeStruct((n_row_k * nv, rank), jnp.float32),
        in_specs=[pl.BlockSpec(memory_space=pl.ANY)] * 4,
        out_specs=pl.BlockSpec(memory_space=pltpu.VMEM),
        scratch_shapes=[
            pltpu.VMEM((total + n_row_k, nv, rank), jnp.bfloat16),
            pltpu.VMEM((per_owner, rank, rank), jnp.bfloat16),
            pltpu.SMEM((1, total), jnp.int32),
            pltpu.SMEM((n_row_k, total), jnp.int32),
            pltpu.SMEM((total + 1,), jnp.int32),
            pltpu.SemaphoreType.DMA((4,)),
            pltpu.SemaphoreType.DMA((per_owner,)),
        ],
        compiler_params=pltpu.CompilerParams(vmem_limit_bytes=40 * 2**20),
    )(qmap, mask, vecs, screened)


def per_device(coeffs, trial, screened, qmap, mask):
    n_col = lax.axis_size("col")
    vec = jnp.einsum("vu,ru->vr", trial[0], coeffs[0], preferred_element_type=jnp.float32)
    vecs = lax.all_gather(vec.astype(jnp.bfloat16), ("row", "col"))
    partial = apply(qmap, mask, vecs, screened, n_col)
    partial = partial.reshape(n_col, vec.shape[0], vec.shape[1])
    own = lax.psum_scatter(partial, "col", scatter_dimension=0)
    high = own.astype(jnp.bfloat16)
    low = (own - high.astype(jnp.float32)).astype(jnp.bfloat16)
    out = jnp.einsum("vr,rt->vt", high, coeffs[0], preferred_element_type=jnp.float32)
    out += jnp.einsum("vr,rt->vt", low, coeffs[0], preferred_element_type=jnp.float32)
    return out[None]


def solution(mesh):
    return jax.shard_map(
        per_device,
        mesh=mesh,
        in_specs=(
            P(("row", "col"), None, None),
            P(("row", "col"), None, None),
            P("col", None, None),
            P(),
            P(),
        ),
        out_specs=P(("row", "col"), None, None),
        check_vma=False,
    )
```

time: 707 us -> 165 us (0.23)
  blocking collectives: 227 us -> 0 us
  waiting for transfers between devices: 253 us -> 131 us
  local copies, waits for them, and re-layouts: 107 us -> 6.95 us
  matrix products: 69.6 us -> 4.1 us
  other arithmetic: 27.6 us -> 0 us
  Pallas kernels: 0 us -> 9.79 us
    all_gather x1 -> x0, blocking collectives: 205 us -> none  [from_root(): lax.all_gather(shard, axis)]
    all_gather x2 -> x1, waiting for transfers between devices: 253 us -> 70.6 us  [per_device(): vecs = lax.all_gather(vec.astype(jnp.bfloat16), ('row', 'col'))]
    gather x17 -> x0, local copies, waits for them, and re-layouts: 94.4 us -> none  [the longest x16 80.1 us: sweep(): picked = jnp.take(received, slots, axis=0)]
    dot_general x32 -> x3, matrix products: 69.6 us -> 4.1 us  [the longest x1 1.66 us: per_device(): jnp.einsum('vr,rt->vt', low, coeffs[0], preferred_element_type=jnp.float32)]
    reduce_scatter x0 -> x1, waiting for transfers between devices: none -> 60 us  [per_device(): own = lax.psum_scatter(partial, 'col', scatter_dimension=0)]
    select_n x18 -> x0, other arithmetic: 23.2 us -> none  [the longest x2 22.8 us: pack_slots(): parcel = jnp.take(screened, source.reshape(-1), axis=0)]
    all_to_all x1 -> x0, blocking collectives: 22.6 us -> none  [sent_and_summed(): lax.all_to_all(in_blocks(shard, dim, devices), axis, 0, 0, tiled=True)]
    pallas_call x0 -> x1, Pallas kernels: none -> 9.79 us  [apply(): pl.pallas_call(lambda *refs: apply_kernel(n_row_k, per_owner, *refs), out...]
  transfers between devices with their start and end apart: 3 -> 2, of which waited for: 2 -> 2; matrix products, arithmetic and copies ran while one was open for 1% -> 0% of each run, Pallas kernels for 0% -> 0%
where the time goes in v1:
time: 165 us
  waiting for transfers between devices  131 us (79%)
  between operations  13.4 us (8%)
  Pallas kernels  9.79 us (6%)
  local copies, waits for them, and re-layouts  6.95 us (4%)
  matrix products  4.1 us (2%)
    all_gather x1, waiting for transfers between devices, per_device(): vecs = lax.all_gather(vec.astype(jnp.bfloat16), ('row', 'col'))  70.6 us
    reduce_scatter x1, waiting for transfers between devices, per_device(): own = lax.psum_scatter(partial, 'col', scatter_dimension=0)  60 us
    pallas_call x1, Pallas kernels, apply(): pl.pallas_call(lambda *refs: apply_kernel(n_row_k, per_owner, *refs), out...  9.79 us
    unnamed x10, local copies, waits for them, and re-layouts  6.95 us
  transfers between devices with their start and end apart: 2, of which 2 were waited for; matrix products, arithmetic and copies ran while one was open for 0% of the time, Pallas kernels for 0%

profile of v1, /device:TPU:0, one launch (start us, length us, event | category | flops | bytes accessed | tf_op | source)
XLA Modules:
  0.0 164.9 jit_solution(17589108818368419700)
XLA Ops:
  6.5 0.0 copy-start
  6.5 0.0 all-gather.3.cloned.1.call-start
  6.5 0.9 copy-done
  7.4 1.5 convolution_convert_fusion
  8.9 0.0 all-gather.3.cloned.1.call-update
  8.9 0.0 reduce-scatter.2.cloned.1.call-start
  9.0 70.6 %all-gather.3.cloned.1.call-done = bf16[4096,512]{1,0:T(8,128)(2,1)} async-done(((bf16[32,512]{1,0:T(8,128)(2,1)}), bf16[4096,512]{1,0:T(8,128)(2,1)}) %all-gather.3.cloned.1.call-update) | async-done | bytes 4194320 | tf_op jit(solution)/shard_map/all_gather | solution.py:93
  79.5 0.0 copy-start.1
  79.5 2.2 %copy-done.1 = bf16[8,512,512]{2,1,0:T(8,128)(2,1)S(1)} copy-done((bf16[8,512,512]{2,1,0:T(8,128)(2,1)S(1)}, bf16[8,512,512]{2,1,0:T(8,128)(2,1)}, u32[]{:S(2)}) %copy-start.1) | copy-done | bytes 4194328
  81.7 0.0 copy-start.2
  81.7 2.2 %copy-done.2 = bf16[4096,512]{1,0:T(8,128)(2,1)S(1)} copy-done((bf16[4096,512]{1,0:T(8,128)(2,1)S(1)}, bf16[4096,512]{1,0:T(8,128)(2,1)}, u32[]{:S(2)}) %copy-start.2) | copy-done | bytes 4194328
  83.9 0.0 copy-start.3
  83.9 0.8 copy-done.3
  84.8 0.0 copy-start.4
  84.8 0.8 copy-done.4
  85.6 9.8 %shard_map.55 = f32[512,512]{1,0:T(8,128)} custom-call(s32[128,128]{1,0:T(8,128)S(1)} %copy-done.3, s32[128,128]{1,0:T(8,128)S(1)} %copy-done.4, bf16[128,32,512]{2,1,0:T(8,128)(2,1)S(1)} %bitcast.20, bf16[8,512,512]{2,1,0:T(8,128)(2,1)S(1)} %copy-done.1), custom_call_target="tpu_custom_call" | custom-call | tf_op jit(solution)/shard_map/pallas_call | solution.py:72
  95.4 0.0 reduce-scatter.2.cloned.1.call-update
  95.4 60.0 %reduce-scatter.2.cloned.1.call-done = f32[1,32,512]{2,1,0:T(8,128)} async-done(((f32[16,32,512]{2,1,0:T(8,128)}), f32[1,32,512]{2,1,0:T(8,128)}) %reduce-scatter.2.cloned.1.call-update) | async-done | bytes 65552 | tf_op jit(solution)/shard_map/reduce_scatter | solution.py:96
  155.4 1.0 fusion.2
  156.4 1.7 %fusion = f32[1,32,128]{2,1,0:T(8,128)} fusion(f32[32,128]{1,0:T(8,128)S(1)} %fusion.2, bf16[1,512,128]{2,1,0:T(8,128)(2,1)S(1)} %copy-done, f32[1,32,512]{2,1,0:T(8,128)} %reduce-scatter.2.cloned.1.call-done), kind=kOutput, calls=%fused_computation.2 | convolution fusion | flops 4263936 | bytes 229376 | tf_op jit(solution)/shard_map/vr,rt->vt/dot_general | solution.py:100
Async XLA Ops:
  6.5 0.9 copy-start
  6.5 73.0 %all-gather.3.cloned.1.call-start = ((), (), s32[]{:S(2)}) async-start(), calls=%async_computation.2 | async-start | bytes 4227072 | tf_op jit(solution)/shard_map/all_gather | solution.py:93
  8.9 146.5 %reduce-scatter.2.cloned.1.call-start = ((), (), s32[]{:S(2)}) async-start(), calls=%async_computation.1 | async-start | bytes 1114112 | tf_op jit(solution)/shard_map/reduce_scatter | solution.py:96
  79.5 2.2 %copy-start.1 = (bf16[8,512,512]{2,1,0:T(8,128)(2,1)S(1)}, bf16[8,512,512]{2,1,0:T(8,128)(2,1)}, u32[]{:S(2)}) copy-start(bf16[8,512,512]{2,1,0:T(8,128)(2,1)} %refs_3_.1) | copy-start | bytes 12582916
  81.7 2.2 %copy-start.2 = (bf16[4096,512]{1,0:T(8,128)(2,1)S(1)}, bf16[4096,512]{1,0:T(8,128)(2,1)}, u32[]{:S(2)}) copy-start(bf16[4096,512]{1,0:T(8,128)(2,1)} %all-gather.3.cloned.1.call-done) | copy-start | bytes 12582916
  83.9 0.8 copy-start.3
  84.8 0.8 copy-start.4
Sparse Core Ops, SparseCore 0:
  10.5 69.0 all-gather.2
  95.5 59.8 reduce-scatter.1

commit v2 on v1

v2 whole, which is shorter than its diff:
```python
import jax
import jax.numpy as jnp
from jax import lax
from jax.experimental import pallas as pl
from jax.experimental.pallas import tpu as pltpu
from jax.sharding import PartitionSpec as P


def apply_kernel(n_row_k, per_owner, qrow_hbm, mask_hbm, vecs, w_ref, out_ref,
                 qrow, masks, found, sems):
    total, nv, rank = vecs.shape
    row_pos = lax.axis_index("row")
    col_pos = lax.axis_index("col")
    k0 = row_pos * n_row_k
    copies = [
        pltpu.make_async_copy(qrow_hbm.at[pl.ds(0, 1)], qrow, sems.at[0]),
        pltpu.make_async_copy(mask_hbm.at[pl.ds(k0, n_row_k)], masks, sems.at[1]),
    ]
    for copy in copies:
        copy.start()
    out_ref[...] = jnp.zeros_like(out_ref)
    for copy in copies:
        copy.wait()

    def scan(d, count):
        q = qrow[0, lax.rem(total - d, total)]
        found[count] = d
        return count + (q // per_owner == col_pos).astype(jnp.int32)

    count = lax.fori_loop(0, total, scan, jnp.int32(0))

    def side(start, weights):
        blocks = []
        for i in range(n_row_k):
            scale = jnp.full((nv, rank), weights[i], jnp.float32).astype(jnp.bfloat16)
            blocks.append(vecs[lax.rem(start + i, total)] * scale)
        return jnp.concatenate(blocks, axis=0)

    def step(j, carry):
        d = found[j]
        q = qrow[0, lax.rem(total - d, total)]
        w = w_ref[q - col_pos * per_owner]
        ahead, behind = [], []
        for i in range(n_row_k):
            ahead.append(masks[i, lax.rem(k0 + i + total - d, total)].astype(jnp.float32))
            mirror = 1 - masks[i, lax.rem(k0 + i + d, total)]
            behind.append(jnp.where(d == 0, 0, mirror).astype(jnp.float32))
        direct = side(k0 + total - d, ahead)
        out_ref[...] += lax.dot_general(
            direct, w, (((1,), (1,)), ((), ())), preferred_element_type=jnp.float32
        )
        turned = side(k0 + d, behind)
        out_ref[...] += jnp.dot(turned, w, preferred_element_type=jnp.float32)
        return carry

    lax.fori_loop(0, count, step, 0)


def apply(qmap, mask, vecs, screened, n_row_k):
    total, nv, rank = vecs.shape
    per_owner = screened.shape[0]
    vmem = pl.BlockSpec(memory_space=pltpu.VMEM)
    return pl.pallas_call(
        lambda *refs: apply_kernel(n_row_k, per_owner, *refs),
        out_shape=jax.ShapeDtypeStruct((n_row_k * nv, rank), jnp.float32),
        in_specs=[pl.BlockSpec(memory_space=pl.ANY)] * 2 + [vmem] * 2,
        out_specs=vmem,
        scratch_shapes=[
            pltpu.SMEM((1, total), jnp.int32),
            pltpu.SMEM((n_row_k, total), jnp.int32),
            pltpu.SMEM((total + 1,), jnp.int32),
            pltpu.SemaphoreType.DMA((2,)),
        ],
        compiler_params=pltpu.CompilerParams(vmem_limit_bytes=24 * 2**20),
    )(qmap, mask, vecs, screened)


MESH = pl.DeviceIdType.MESH
SIDE = 4
PARTS = (
    ((0, 16), (0, 384), "yzx"),
    ((16, 16), (0, 384), "xzy"),
    ((0, 32), (384, 128), "xyz"),
)


def position():
    row, col = lax.axis_index("row"), lax.axis_index("col")
    return {"x": row // 2, "z": row % 2 * 2 + col // 8, "y": col % 8 // 2}, col % 2


def device(at, core):
    return (at["x"] * 2 + at["z"] // 2, at["z"] % 2 * 8 + at["y"] * 2 + core)


def moved(at, dim, by):
    return {**at, dim: lax.rem(at[dim] + SIDE + by, SIDE)}


def greet(peers):
    barrier = pltpu.get_barrier_semaphore()
    for peer in peers:
        pl.semaphore_signal(barrier, inc=1, device_id=peer, device_id_type=MESH)
    pl.semaphore_wait(barrier, len(peers))


def gather_kernel(coeffs, trial, buf, own, local_sem, send_sems, recv_sems):
    at, core = position()
    own[...] = lax.dot_general(
        trial[0], coeffs[0], (((1,), (1,)), ((), ())), preferred_element_type=jnp.float32
    ).astype(own.dtype)
    greet([device(moved(at, dim, by), core) for dim in "xyz" for by in (1, -1)] + [device(at, 1 - core)])
    started = []

    def push(src, dst, to):
        k = len(started)
        copy = pltpu.make_async_remote_copy(
            src, dst, send_sems.at[k], recv_sems.at[k], device_id=to, device_id_type=MESH
        )
        copy.start()
        started.append(copy)
        return copy

    def region(spans, part):
        rows, cols, _ = part
        return buf.at[
            pl.ds(*spans["x"]), pl.ds(*spans["z"]), pl.ds(*spans["y"]), core, pl.ds(*rows), pl.ds(*cols)
        ]

    here = buf.at[at["x"], at["z"], at["y"], core]
    keep = pltpu.make_async_copy(own, here, local_sem)
    keep.start()
    first = {}
    for part in PARTS:
        rows, cols, order = part
        piece = own.at[pl.ds(*rows), pl.ds(*cols)]
        target = here.at[pl.ds(*rows), pl.ds(*cols)]
        first[part] = tuple(push(piece, target, device(moved(at, order[0], by), core)) for by in (1, -1))
    shared = [push(own, here, device(at, 1 - core))]
    keep.wait()
    for stage in range(3):
        waiting = {}
        for part in PARTS:
            order = part[2]
            dim = order[stage]
            if stage == 0:
                waiting[part] = first[part]
                continue
            spans = {d: (0, SIDE) if d in order[:stage] else (at[d], 1) for d in "xyz"}
            block = region(spans, part)
            waiting[part] = tuple(push(block, block, device(moved(at, dim, by), core)) for by in (1, -1))
        relays = {}
        for part in PARTS:
            order = part[2]
            dim = order[stage]
            up, down = (device(moved(at, dim, by), core) for by in (1, -1))
            spans = {d: (0, SIDE) if d in order[:stage] else (at[d], 1) for d in "xyz"}
            before = {**spans, dim: (moved(at, dim, -1)[dim], 1)}
            after = {**spans, dim: (moved(at, dim, 1)[dim], 1)}
            half = [before, after]
            if stage > 0:
                half = [{**before, order[0]: (0, SIDE // 2)}, {**after, order[0]: (SIDE // 2, SIDE // 2)}]
            waiting[part][0].wait_recv()
            block = region(half[0], part)
            relays[part] = [push(block, block, up)]
            waiting[part][1].wait_recv()
            if stage > 0:
                block = region(half[1], part)
                relays[part].append(push(block, block, down))
            for spans in (before, after):
                block = region(spans, part)
                shared.append(push(block, block, device(at, 1 - core)))
        for part in PARTS:
            order = part[2]
            dim = order[stage]
            spans = {d: (0, SIDE) if d in order[:stage] else (at[d], 1) for d in "xyz"}
            for copy in relays[part]:
                copy.wait_recv()
            block = region({**spans, dim: (moved(at, dim, 2)[dim], 1)}, part)
            shared.append(push(block, block, device(at, 1 - core)))
    for copy in shared:
        copy.wait_recv()
    for copy in started:
        copy.wait_send()


def gather(coeffs, trial):
    nv, rank = trial.shape[1], coeffs.shape[1]
    copies = 61
    vmem = pl.BlockSpec(memory_space=pltpu.VMEM)
    return pl.pallas_call(
        gather_kernel,
        out_shape=jax.ShapeDtypeStruct((SIDE, SIDE, SIDE, 2, nv, rank), jnp.bfloat16),
        in_specs=[vmem, vmem],
        out_specs=pl.BlockSpec(memory_space=pl.ANY),
        scratch_shapes=[
            pltpu.VMEM((nv, rank), jnp.bfloat16),
            pltpu.SemaphoreType.DMA,
            pltpu.SemaphoreType.DMA((copies,)),
            pltpu.SemaphoreType.DMA((copies,)),
        ],
        compiler_params=pltpu.CompilerParams(
            collective_id=0, has_side_effects=True, vmem_limit_bytes=4 * 2**20
        ),
    )(coeffs, trial)


def reduce_kernel(partial, coeffs, out, pair, staged, landed, pair_send, pair_recv, send_sems, recv_sems):
    at, core = position()
    zl, y = at["z"] % 2, at["y"]
    row = lax.axis_index("row")
    steps = [(a, b) for b in (2, 1, 3, 0) for a in (1, 0)]

    def there(a, b):
        return lax.rem(zl + a, 2), lax.rem(y + b, SIDE)

    def peer(a, b, c):
        far_z, far_y = there(a, b)
        return (row, far_z * 8 + far_y * 2 + c)

    greet([peer(a, b, core) for a, b in steps if (a, b) != (0, 0)] + [peer(0, 0, 1 - core)])
    swaps = []
    for k, (a, b) in enumerate(steps):
        far_z, far_y = there(a, b)
        swap = pltpu.make_async_remote_copy(
            partial.at[far_z, far_y, 1 - core], pair.at[k], pair_send.at[k], pair_recv.at[k],
            device_id=peer(0, 0, 1 - core), device_id_type=MESH,
        )
        swap.start()
        swaps.append(swap)
    sends = []

    def post(k):
        send = pltpu.make_async_remote_copy(
            staged.at[k], landed.at[k], send_sems.at[k], recv_sems.at[k],
            device_id=peer(*steps[k], core), device_id_type=MESH,
        )
        send.start()
        sends.append(send)

    total = None
    for k, (a, b) in enumerate(steps):
        far_z, far_y = there(a, b)
        swaps[k].wait_recv()
        both = partial[far_z, far_y, core] + pair[k]
        if (a, b) == (0, 0):
            total = both
        else:
            staged[k] = both.astype(staged.dtype)
        if k > 0:
            post(k - 1)
    for k, send in enumerate(sends):
        send.wait_recv()
        total += landed[k].astype(jnp.float32)
    high = total.astype(jnp.bfloat16)
    low = (total - high.astype(jnp.float32)).astype(jnp.bfloat16)
    out[0] = jnp.dot(high, coeffs[0], preferred_element_type=jnp.float32) + jnp.dot(
        low, coeffs[0], preferred_element_type=jnp.float32
    )
    for copy in swaps + sends:
        copy.wait_send()


def reduce(partial, coeffs):
    nv, rank, nt = partial.shape[-2], partial.shape[-1], coeffs.shape[2]
    vmem = pl.BlockSpec(memory_space=pltpu.VMEM)
    return pl.pallas_call(
        reduce_kernel,
        out_shape=jax.ShapeDtypeStruct((1, nv, nt), jnp.float32),
        in_specs=[vmem, vmem],
        out_specs=vmem,
        scratch_shapes=[
            pltpu.VMEM((8, nv, rank), jnp.float32),
            pltpu.VMEM((7, nv, rank), jnp.bfloat16),
            pltpu.VMEM((7, nv, rank), jnp.bfloat16),
            pltpu.SemaphoreType.DMA((8,)),
            pltpu.SemaphoreType.DMA((8,)),
            pltpu.SemaphoreType.DMA((7,)),
            pltpu.SemaphoreType.DMA((7,)),
        ],
        compiler_params=pltpu.CompilerParams(
            collective_id=1, has_side_effects=True, vmem_limit_bytes=8 * 2**20
        ),
    )(partial, coeffs)


def per_device(coeffs, trial, screened, qmap, mask):
    n_col = lax.axis_size("col")
    nv, rank = trial.shape[1], coeffs.shape[1]
    vecs = gather(coeffs, trial).reshape(-1, nv, rank)
    partial = apply(qmap, mask, vecs, screened, n_col)
    return reduce(partial.reshape(2, SIDE, 2, nv, rank), coeffs)


def solution(mesh):
    return jax.shard_map(
        per_device,
        mesh=mesh,
        in_specs=(
            P(("row", "col"), None, None),
            P(("row", "col"), None, None),
            P("col", None, None),
            P(),
            P(),
        ),
        out_specs=P(("row", "col"), None, None),
        check_vma=False,
    )
```

time: 165 us -> 54.7 us (0.33)
  waiting for transfers between devices: 131 us -> 0 us
  Pallas kernels: 9.79 us -> 51.4 us
  between operations: 13.4 us -> 0.07 us
  local copies, waits for them, and re-layouts: 6.95 us -> 2.64 us
  matrix products: 4.1 us -> 0 us
    all_gather x1 -> x0, waiting for transfers between devices: 70.6 us -> none  [per_device(): vecs = lax.all_gather(vec.astype(jnp.bfloat16), ('row', 'col'))]
    reduce_scatter x1 -> x0, waiting for transfers between devices: 60 us -> none  [per_device(): own = lax.psum_scatter(partial, 'col', scatter_dimension=0)]
    pallas_call x0 -> x2, Pallas kernels: none -> 42.6 us  [the longest x1 33 us: gather(): pl.pallas_call(gather_kernel, out_shape=jax.ShapeDtypeStruct((SIDE, SIDE,...]
    unnamed x10 -> x13, local copies, waits for them, and re-layouts: 6.95 us -> 2.64 us
    dot_general x3 -> x0, matrix products: 4.1 us -> none  [the longest x1 1.66 us: per_device(): jnp.einsum('vr,rt->vt', low, coeffs[0], preferred_element_type=jnp.float32)]
  transfers between devices with their start and end apart: 2 -> 0, of which waited for: 2 -> 0; matrix products, arithmetic and copies ran while one was open for 0% -> 0% of each run, Pallas kernels for 0% -> 0%
where the time goes in v2:
time: 54.7 us; the launch traced here: 54.1 us
  Pallas kernels  51.4 us (94%)
  local copies, waits for them, and re-layouts  2.64 us (5%)
    pallas_call x1, Pallas kernels, gather(): pl.pallas_call(gather_kernel, out_shape=jax.ShapeDtypeStruct((SIDE, SIDE,...  33 us
    pallas_call x1, Pallas kernels, reduce(): pl.pallas_call(reduce_kernel, out_shape=jax.ShapeDtypeStruct((1, nv, nt),...  9.61 us
    pallas_call x1, Pallas kernels, apply(): pl.pallas_call(lambda *refs: apply_kernel(n_row_k, per_owner, *refs), out...  8.73 us
    unnamed x13, local copies, waits for them, and re-layouts  2.64 us

profile of v2, /device:TPU:0, one launch (start us, length us, event | category | flops | bytes accessed | tf_op | source)
XLA Modules:
  0.0 54.1 jit_solution(14807174407248635997)
XLA Ops:
  0.0 0.0 copy-start
  0.0 0.0 copy-start.1
  0.0 1.1 %copy-done.1 = bf16[1,512,128]{2,1,0:T(8,128)(2,1)S(1)} copy-done((bf16[1,512,128]{2,1,0:T(8,128)(2,1)S(1)}, bf16[1,512,128]{2,1,0:T(8,128)(2,1)}, u32[]{:S(2)}) %copy-start.1) | copy-done | bytes 131096
  1.1 0.0 copy-start.5
  1.1 1.0 %copy-done.5 = bf16[1,32,128]{2,1,0:T(8,128)(2,1)S(1)} copy-done((bf16[1,32,128]{2,1,0:T(8,128)(2,1)S(1)}, bf16[1,32,128]{2,1,0:T(8,128)(2,1)}, u32[]{:S(2)}) %copy-start.5) | copy-done | bytes 8216
  2.0 0.0 copy-start.3
  2.0 0.0 copy-start.4
  2.0 33.0 %shard_map.55 = bf16[4,4,4,2,32,512]{5,4,3,2,1,0:T(8,128)(2,1)S(1)} custom-call(bf16[1,512,128]{2,1,0:T(8,128)(2,1)S(1)} %copy-done.1, bf16[1,32,128]{2,1,0:T(8,128)(2,1)S(1)} %copy-done.5), custom_call_target="tpu_custom_call" | custom-call | tf_op jit(solution)/shard_map/pallas_call | solution.py:191
  35.0 0.0 copy-done
  35.1 0.0 copy-done.3
  35.1 0.0 copy-done.4
  35.1 0.0 copy-start.2
  35.1 8.7 %shard_map.56 = f32[512,512]{1,0:T(8,128)S(1)} custom-call(s32[128,128]{1,0:T(8,128)S(1)} %copy-done.3, s32[128,128]{1,0:T(8,128)S(1)} %copy-done.4, bf16[128,32,512]{2,1,0:T(8,128)(2,1)S(1)} %bitcast.2, bf16[8,512,512]{2,1,0:T(8,128)(2,1)S(1)} %copy-done), custom_call_target="tpu_custom_call" | custom-call | tf_op jit(solution)/shard_map/pallas_call | solution.py:63
  43.8 0.0 copy-done.2
  43.8 9.6 %shard_map.57 = f32[1,32,128]{2,1,0:T(8,128)S(1)} custom-call(f32[2,4,2,32,512]{4,3,2,1,0:T(8,128)S(1)} %bitcast.3, bf16[1,512,128]{2,1,0:T(8,128)(2,1)S(1)} %copy-done.2), custom_call_target="tpu_custom_call" | custom-call | tf_op jit(solution)/shard_map/pallas_call | solution.py:267
  53.5 0.6 %copy.7 = f32[1,32,128]{2,1,0:T(8,128)} copy(f32[1,32,128]{2,1,0:T(8,128)S(1)} %shard_map.57) | data formatting | bytes 32768
Async XLA Ops:
  0.0 35.0 %copy-start = (bf16[8,512,512]{2,1,0:T(8,128)(2,1)S(1)}, bf16[8,512,512]{2,1,0:T(8,128)(2,1)}, u32[]{:S(2)}) copy-start(bf16[8,512,512]{2,1,0:T(8,128)(2,1)} %refs_3_.1) | copy-start | bytes 12582916
  0.0 1.1 %copy-start.1 = (bf16[1,512,128]{2,1,0:T(8,128)(2,1)S(1)}, bf16[1,512,128]{2,1,0:T(8,128)(2,1)}, u32[]{:S(2)}) copy-start(bf16[1,512,128]{2,1,0:T(8,128)(2,1)} %coeffs.3) | copy-start | bytes 393220
  1.1 1.0 %copy-start.5 = (bf16[1,32,128]{2,1,0:T(8,128)(2,1)S(1)}, bf16[1,32,128]{2,1,0:T(8,128)(2,1)}, u32[]{:S(2)}) copy-start(bf16[1,32,128]{2,1,0:T(8,128)(2,1)} %trial.1) | copy-start | bytes 24580
  2.0 33.0 %copy-start.3 = (s32[128,128]{1,0:T(8,128)S(1)}, s32[128,128]{1,0:T(8,128)}, u32[]{:S(2)}) copy-start(s32[128,128]{1,0:T(8,128)} %refs_0_.1) | copy-start | bytes 196612
  2.0 33.0 %copy-start.4 = (s32[128,128]{1,0:T(8,128)S(1)}, s32[128,128]{1,0:T(8,128)}, u32[]{:S(2)}) copy-start(s32[128,128]{1,0:T(8,128)} %refs_1_.1) | copy-start | bytes 196612
  35.1 8.8 %copy-start.2 = (bf16[1,512,128]{2,1,0:T(8,128)(2,1)S(1)}, bf16[1,512,128]{2,1,0:T(8,128)(2,1)}, u32[]{:S(2)}) copy-start(bf16[1,512,128]{2,1,0:T(8,128)(2,1)} %coeffs.3) | copy-start | bytes 393220

commit v3 on v1

v3 whole, which is shorter than its diff:
```python
import jax
import jax.numpy as jnp
from jax import lax
from jax.experimental import pallas as pl
from jax.experimental.pallas import tpu as pltpu
from jax.sharding import PartitionSpec as P


MESH = pl.DeviceIdType.MESH
SIDE = 4
PARTS = (
    ((0, 16), (0, 384), "yzx"),
    ((16, 16), (0, 384), "zxy"),
    ((0, 32), (384, 128), "xyz"),
)
NEAR = (0, 1, -1, 2)
UP, DOWN = (0, 2), (1, -1)


def position():
    row, col = lax.axis_index("row"), lax.axis_index("col")
    return {"x": row // 2, "z": row % 2 * 2 + col // 8, "y": col % 8 // 2}, col % 2


def device(at, core):
    return (at["x"] * 2 + at["z"] // 2, at["z"] % 2 * 8 + at["y"] * 2 + core)


def moved(at, dim, by):
    return {**at, dim: lax.rem(at[dim] + SIDE + by, SIDE)}


def greet(peers):
    barrier = pltpu.get_barrier_semaphore()
    for peer in peers:
        pl.semaphore_signal(barrier, inc=1, device_id=peer, device_id_type=MESH)
    return lambda: pl.semaphore_wait(barrier, len(peers))


def one_round(n_slots, n_row_k, turn, coeffs_hbm, trial_hbm, w_hbm, q_hbm, mask_hbm, out, most,
              coeffs, trial, own, part0, part1, part2, vecs, weights, acc, pair, staged, landed,
              qrow, qvec, masks, slots, load_sems, local_sems, send_sems, recv_sems):
    at, core = position()
    partner = device(at, 1 - core)
    row, col = lax.axis_index("row"), lax.axis_index("col")
    zl, y = at["z"] % 2, at["y"]
    spread = [(a, b) for b in (2, 1, 3, 0) for a in (1, 0)]

    def there(a, b):
        return lax.rem(zl + a, 2), lax.rem(y + b, SIDE)

    def peer(a, b):
        far_z, far_y = there(a, b)
        return (row, far_z * 8 + far_y * 2 + core)

    meet = greet(
        [device(moved(at, dim, by), core) for dim in "xyz" for by in (1, -1, 2)]
        + [partner] + [peer(1, b) for b in (1, 2, 3)]
    )
    k0 = row * n_row_k
    total = q_hbm.shape[1]
    rows = mask_hbm.at[pl.ds(k0, n_row_k)]
    loads = [
        pltpu.make_async_copy(coeffs_hbm, coeffs, load_sems.at[0]),
        pltpu.make_async_copy(trial_hbm, trial, load_sems.at[1]),
        pltpu.make_async_copy(q_hbm.at[pl.ds(0, 1)], qrow, load_sems.at[2]),
        pltpu.make_async_copy(rows, masks.at[:, pl.ds(0, total)], load_sems.at[3]),
        pltpu.make_async_copy(rows, masks.at[:, pl.ds(total, total)], load_sems.at[4]),
        pltpu.make_async_copy(w_hbm, weights, load_sems.at[5]),
        pltpu.make_async_copy(q_hbm.at[pl.ds(0, 1)], qvec, load_sems.at[6]),
    ]
    for load in loads:
        load.start()
    for load in loads[:2]:
        load.wait()
    own[...] = lax.dot_general(
        trial[0], coeffs[0], (((1,), (1,)), ((), ())), preferred_element_type=jnp.float32
    ).astype(own.dtype)
    bufs = (part0, part1, part2)
    started, shared, local = [], [], []
    arrivals = {}

    def push(src, dst, to):
        k = len(started)
        copy = pltpu.make_async_remote_copy(
            src, dst, send_sems.at[k], recv_sems.at[k], device_id=to, device_id_type=MESH
        )
        copy.start()
        started.append(copy)
        return copy

    def keep(src, dst):
        copy = pltpu.make_async_copy(src, dst, local_sems.at[len(local)])
        copy.start()
        local.append(copy)

    def coords(n, steps):
        order = PARTS[n][2]
        return {d: None if by is None else moved(at, d, by)[d] for d, by in zip(order, steps)}

    def region(n, steps):
        place = coords(n, steps)
        return bufs[n].at[tuple(place[d] for d in PARTS[n][2][::-1] if place[d] is not None)]

    def final(n, steps):
        place = coords(n, steps)
        rows, cols = PARTS[n][:2]
        spans = tuple(pl.ds(0, SIDE) if place[d] is None else place[d] for d in "xzy")
        return vecs.at[spans + (core, pl.ds(*rows), pl.ds(*cols))]

    def place(n, steps):
        src, dst = region(n, steps), final(n, steps)
        shared.append(push(src, dst, partner))
        keep(src, dst)

    def send(n, stage, by, steps, src=None):
        dim = PARTS[n][2][stage]
        block = region(n, steps)
        copy = push(block if src is None else src, block, device(moved(at, dim, by), core))
        came = list(steps)
        came[stage] = (steps[stage] - by + 1) % SIDE - 1
        arrivals[n, tuple(came)] = copy

    def arrived(n, steps):
        arrivals[n, steps].wait_recv()

    def prepare():
        for load in loads[2:5]:
            load.wait()
        base = col * n_slots
        skip = turn[0] * n_slots

        def scan(j, carry):
            count, picked = carry
            q = qrow[0, j]
            held = (q >= base) & (q < base + n_slots)
            picked = tuple(jnp.where(held & (count == n), j, p) for n, p in enumerate(picked))
            return count + jnp.where(held, 1, 0), picked

        first = (-skip, (jnp.int32(-1),) * n_slots)
        _, picked = lax.fori_loop(0, total, scan, first, unroll=4)
        for n, p in enumerate(picked):
            slots[n] = p
        acc[...] = jnp.zeros_like(acc)
        loads[6].wait()
        first_q = n_slots * lax.broadcasted_iota(jnp.int32, (n_row_k, total), 0)
        held = (qvec[...] >= first_q) & (qvec[...] < first_q + n_slots)
        counts = jnp.sum(jnp.where(held, 1.0, 0.0), axis=1, keepdims=True)
        most[0] = jnp.max(counts).astype(jnp.int32)

    parts = range(len(PARTS))
    own_piece = [own.at[pl.ds(*PARTS[n][0]), pl.ds(*PARTS[n][1])] for n in parts]
    for n in parts:
        keep(own_piece[n], region(n, (0, 0, 0)))
    meet()
    for by in (2, 1, -1):
        for n in parts:
            send(n, 0, by, (0, 0, 0), own_piece[n])
    for by in (2, 1, -1):
        for n in parts:
            send(n, 1, by, (0, 0, 0), own_piece[n])
    for copy in local:
        copy.wait()
    del local[:]
    for near in (1, -1, 2):
        for n in parts:
            arrived(n, (near, 0, 0))
            for by in (2, 1, -1):
                send(n, 1, by, (near, 0, 0))
    for near in NEAR:
        for n in parts:
            if near != 0:
                for first in NEAR:
                    arrived(n, (first, near, 0))
            for by in (1, -1):
                send(n, 2, by, (None, near, 0))
            place(n, (None, near, 0))
    prepare()
    for near in NEAR:
        for n in parts:
            for by in (1, -1):
                arrived(n, (None, near, -by))
                if near in (UP if by == 1 else DOWN):
                    send(n, 2, by, (None, near, -by))
                place(n, (None, near, -by))
    for near in NEAR:
        for n in parts:
            arrived(n, (None, near, 2))
            place(n, (None, near, 2))
    for copy in shared:
        copy.wait_recv()
    for copy in local:
        copy.wait()
    loads[5].wait()
    nv, rank = own.shape

    def wrapped(k):
        return jnp.where(k >= total, k - total, k)

    def side(start, scales):
        blocks = []
        for i in range(n_row_k):
            scale = jnp.full((nv, rank), scales[i], jnp.float32).astype(own.dtype)
            blocks.append(flat[wrapped(start + i)] * scale)
        return jnp.concatenate(blocks, axis=0)

    flat = vecs.reshape(total, nv, rank)

    def step(n, carry):
        slot = slots[n]
        used = jnp.where(slot >= 0, 1, 0)
        j = jnp.where(slot >= 0, slot, 0)
        w = weights[jnp.where(slot >= 0, qrow[0, j] - col * n_slots, 0)]
        ahead_k = wrapped(k0 + j)
        behind_k = wrapped(k0 + total - j)
        turned_used = jnp.where(slot > 0, 1, 0)
        ahead = [(used * masks[i, ahead_k + i]).astype(jnp.float32) for i in range(n_row_k)]
        behind = [(turned_used * (1 - masks[i, behind_k + i])).astype(jnp.float32) for i in range(n_row_k)]
        direct = side(ahead_k, ahead)
        turned = side(behind_k, behind)
        both = lax.dot_general(
            direct, w, (((1,), (1,)), ((), ())), preferred_element_type=jnp.float32
        ) + jnp.dot(turned, w, preferred_element_type=jnp.float32)
        acc[...] += both.reshape(acc.shape)
        return carry

    lax.fori_loop(0, n_slots, step, 0)

    def mate(k, c):
        far_z, far_y = there(*spread[k])
        return far_z * 8 + far_y * 2 + c

    swaps = [push(acc.at[mate(k, 1 - core)], pair.at[k], partner) for k in range(8)]
    sends = []

    def post(k):
        sends.append(push(staged.at[k], landed.at[k], peer(*spread[k])))

    for k in range(8):
        swaps[k].wait_recv()
        summed = acc[mate(k, core)] + pair[k]
        if k < 7:
            staged[k] = summed.astype(staged.dtype)
        if k > 0:
            post(k - 1)
    for k in range(7):
        sends[k].wait_recv()
        summed += landed[k].astype(jnp.float32)
    high = summed.astype(jnp.bfloat16)
    low = (summed - high.astype(jnp.float32)).astype(jnp.bfloat16)
    out[0] = jnp.dot(high, coeffs[0], preferred_element_type=jnp.float32) + jnp.dot(
        low, coeffs[0], preferred_element_type=jnp.float32
    )
    for copy in started:
        copy.wait_send()


def run_round(turn, coeffs, trial, screened, qmap, mask):
    nv, rank, nt = trial.shape[1], coeffs.shape[1], coeffs.shape[2]
    n_slots = screened.shape[0]
    n_row_k = lax.axis_size("col")
    total = qmap.shape[0]
    pieces, shares = 27 * len(PARTS), 16 * len(PARTS)
    remote = pieces + shares + 15
    anywhere = pl.BlockSpec(memory_space=pl.ANY)
    return pl.pallas_call(
        lambda *refs: one_round(n_slots, n_row_k, *refs),
        out_shape=(
            jax.ShapeDtypeStruct((1, nv, nt), jnp.float32),
            jax.ShapeDtypeStruct((1,), jnp.int32),
        ),
        in_specs=[pl.BlockSpec(memory_space=pltpu.SMEM)] + [anywhere] * 5,
        out_specs=(pl.BlockSpec(memory_space=pltpu.VMEM), pl.BlockSpec(memory_space=pltpu.SMEM)),
        scratch_shapes=[
            pltpu.VMEM(coeffs.shape, coeffs.dtype),
            pltpu.VMEM(trial.shape, trial.dtype),
            pltpu.VMEM((nv, rank), jnp.bfloat16),
        ]
        + [pltpu.VMEM((SIDE, SIDE, SIDE, part[0][1], part[1][1]), jnp.bfloat16) for part in PARTS]
        + [
            pltpu.VMEM((SIDE, SIDE, SIDE, 2, nv, rank), jnp.bfloat16),
            pltpu.VMEM(screened.shape, screened.dtype),
            pltpu.VMEM((n_row_k, nv, rank), jnp.float32),
            pltpu.VMEM((8, nv, rank), jnp.float32),
            pltpu.VMEM((7, nv, rank), jnp.bfloat16),
            pltpu.VMEM((7, nv, rank), jnp.bfloat16),
            pltpu.SMEM((1, total), jnp.int32),
            pltpu.VMEM((1, total), jnp.int32),
            pltpu.SMEM((n_row_k, 2 * total), jnp.int32),
            pltpu.SMEM((n_slots,), jnp.int32),
            pltpu.SemaphoreType.DMA((7,)),
            pltpu.SemaphoreType.DMA((shares,)),
            pltpu.SemaphoreType.DMA((remote,)),
            pltpu.SemaphoreType.DMA((remote,)),
        ],
        compiler_params=pltpu.CompilerParams(
            collective_id=0, has_side_effects=True, vmem_limit_bytes=60 * 2**20
        ),
    )(turn, coeffs, trial, screened, qmap, mask)


def per_device(coeffs, trial, screened, qmap, mask):
    n_slots = screened.shape[0]
    args = (coeffs, trial, screened, qmap, mask)
    first, most = run_round(jnp.zeros((1,), jnp.int32), *args)

    def more(state):
        return state[0] * n_slots < most[0]

    def again(state):
        return state[0] + 1, state[1] + run_round(state[0][None], *args)[0]

    return lax.while_loop(more, again, (jnp.int32(1), first))[1]


def solution(mesh):
    return jax.shard_map(
        per_device,
        mesh=mesh,
        in_specs=(
            P(("row", "col"), None, None),
            P(("row", "col"), None, None),
            P("col", None, None),
            P(),
            P(),
        ),
        out_specs=P(("row", "col"), None, None),
        check_vma=False,
    )
```

time: 165 us -> 41.6 us (0.25)
  waiting for transfers between devices: 131 us -> 0 us
  Pallas kernels: 9.79 us -> 39.7 us
  between operations: 13.4 us -> 0.05 us
  local copies, waits for them, and re-layouts: 6.95 us -> 0.62 us
  matrix products: 4.1 us -> 0 us
    all_gather x1 -> x0, waiting for transfers between devices: 70.6 us -> none  [per_device(): vecs = lax.all_gather(vec.astype(jnp.bfloat16), ('row', 'col'))]
    reduce_scatter x1 -> x0, waiting for transfers between devices: 60 us -> none  [per_device(): own = lax.psum_scatter(partial, 'col', scatter_dimension=0)]
    pallas_call x1, Pallas kernels: 9.79 us -> 39.7 us  [run_round(): pl.pallas_call(lambda *refs: one_round(n_slots, n_row_k, *refs), out_shap...]
    unnamed x10 -> x9, local copies, waits for them, and re-layouts: 6.95 us -> 0.62 us
    dot_general x3 -> x0, matrix products: 4.1 us -> none  [the longest x1 1.66 us: per_device(): jnp.einsum('vr,rt->vt', low, coeffs[0], preferred_element_type=jnp.float32)]
  transfers between devices with their start and end apart: 2 -> 0, of which waited for: 2 -> 0; matrix products, arithmetic and copies ran while one was open for 0% -> 0% of each run, Pallas kernels for 0% -> 0%
where the time goes in v3:
time: 41.6 us; the launch traced here: 40.9 us
  Pallas kernels  39.7 us (95%)
  local copies, waits for them, and re-layouts  0.62 us (1%)
  loops' own time  0.57 us (1%)
    pallas_call x1, Pallas kernels, run_round(): pl.pallas_call(lambda *refs: one_round(n_slots, n_row_k, *refs), out_shap...  39.7 us

profile of v3, /device:TPU:0, one launch (start us, length us, event | category | flops | bytes accessed | tf_op | source)
XLA Modules:
  0.0 40.9 jit_solution(13790381948682775486)
XLA Ops:
  0.0 0.0 copy-start.2
  0.0 0.0 copy-start.1
  0.0 0.0 copy-start.3
  0.0 0.0 copy-start
  0.0 39.7 %shard_map.55 = (f32[1,32,128]{2,1,0:T(8,128)S(1)}, s32[1]{0:T(128)}) custom-call(s32[1]{0:T(128)} %constant.4.clone.1.refs_0_, bf16[1,512,128]{2,1,0:T(8,128)(2,1)} %refs_1_.1, bf16[1,32,128]{2,1,0:T(8,128)(2,1)} %refs_2_.1, bf16[8,512,512]{2,1,0:T(8,128)(2,1)} %refs_3_.1, s32[128,128]{1,0:T(8,128)} %refs_4_.1, s32[128,128]{1,0:T(8,128)} %refs_5_.1), custom_call_target="tpu_custom_call" | custom-call | tf_op jit(solution)/shard_map/pallas_call | solution.py:266
  39.7 0.0 copy-done.2
  39.7 0.0 copy-done.1
  39.7 0.0 copy-done.3
  39.7 0.0 copy-done
  39.7 0.6 %while.10 = (s32[]{:T(128)}, f32[1,32,128]{2,1,0:T(8,128)S(1)}, s32[1]{0:T(128)}, bf16[1,512,128]{2,1,0:T(8,128)(2,1)S(1)}, bf16[1,32,128]{2,1,0:T(8,128)(2,1)S(...) while((s32[]{:T(128)}, f32[1,32,128]{2,1,0:T(8,128)S(1)}, ...), condition=%wide.region_1.0_spmd, body=%wide.region_0.0_spmd.sunk | while | flops 4099 | bytes 49265 | solution.py:313
  40.3 0.6 %copy.13 = f32[1,32,128]{2,1,0:T(8,128)} copy(f32[1,32,128]{2,1,0:T(8,128)S(1)} %get-tuple-element.53) | data formatting | bytes 32768
Async XLA Ops:
  0.0 39.7 %copy-start.2 = (s32[128,128]{1,0:T(8,128)S(1)}, s32[128,128]{1,0:T(8,128)}, u32[]{:S(2)}) copy-start(s32[128,128]{1,0:T(8,128)} %refs_5_.1) | copy-start | bytes 196612
  0.0 39.7 %copy-start.1 = (s32[128,128]{1,0:T(8,128)S(1)}, s32[128,128]{1,0:T(8,128)}, u32[]{:S(2)}) copy-start(s32[128,128]{1,0:T(8,128)} %refs_4_.1) | copy-start | bytes 196612
  0.0 39.7 %copy-start.3 = (bf16[1,32,128]{2,1,0:T(8,128)(2,1)S(1)}, bf16[1,32,128]{2,1,0:T(8,128)(2,1)}, u32[]{:S(2)}) copy-start(bf16[1,32,128]{2,1,0:T(8,128)(2,1)} %refs_2_.1) | copy-start | bytes 24580
  0.0 39.7 %copy-start = (bf16[1,512,128]{2,1,0:T(8,128)(2,1)S(1)}, bf16[1,512,128]{2,1,0:T(8,128)(2,1)}, u32[]{:S(2)}) copy-start(bf16[1,512,128]{2,1,0:T(8,128)(2,1)} %refs_1_.1) | copy-start | bytes 393220

commit v4 on v3

v4 whole, which is shorter than its diff:
```python
import jax
import jax.numpy as jnp
from jax import lax
from jax.experimental import pallas as pl
from jax.experimental.pallas import tpu as pltpu
from jax.sharding import PartitionSpec as P


MESH = pl.DeviceIdType.MESH
SIDE = 4
HALVES = 2
PARTS = tuple(
    (h, (16 * h + r, n), cols, order, dims)
    for h in range(HALVES)
    for r, n, cols, order, dims in (
        (0, 8, (0, 384), "yzx", "xzy"),
        (8, 8, (0, 384), "zxy", "yxz"),
        (0, 16, (384, 128), "xyz", "zxy"),
    )
)


def position():
    row, col = lax.axis_index("row"), lax.axis_index("col")
    return {"x": row // 2, "z": row % 2 * 2 + col // 8, "y": col % 8 // 2}, col % 2


def device(at, core):
    return (at["x"] * 2 + at["z"] // 2, at["z"] % 2 * 8 + at["y"] * 2 + core)


def moved(at, dim, by):
    return {**at, dim: lax.rem(at[dim] + SIDE + by, SIDE)}


def greet(peers):
    barrier = pltpu.get_barrier_semaphore()
    for peer in peers:
        pl.semaphore_signal(barrier, inc=1, device_id=peer, device_id_type=MESH)
    return lambda: pl.semaphore_wait(barrier, len(peers))


def one_round(n_slots, n_row_k, turn, coeffs_hbm, trial_hbm, w_hbm, q_hbm, mask_hbm, out, most,
              coeffs, trial, own, *rest):
    bufs, rest = rest[: len(PARTS)], rest[len(PARTS) :]
    vecs, rest = rest[:HALVES], rest[HALVES:]
    (weights, acc, pair, staged, landed, qrow, qvec, masks, slots,
     load_sems, local_sems, send_sems, recv_sems) = rest
    at, core = position()
    partner = device(at, 1 - core)
    row, col = lax.axis_index("row"), lax.axis_index("col")
    zl, y = at["z"] % 2, at["y"]
    spread = [(a, b) for b in (2, 1, 3, 0) for a in (1, 0)]

    def there(a, b):
        return lax.rem(zl + a, 2), lax.rem(y + b, SIDE)

    def peer(a, b):
        far_z, far_y = there(a, b)
        return (row, far_z * 8 + far_y * 2 + core)

    meet = greet(
        [device(moved(at, dim, by), core) for dim in "xyz" for by in (1, -1, 2)]
        + [partner] + [peer(1, b) for b in (1, 2, 3)]
    )
    k0 = row * n_row_k
    total = q_hbm.shape[1]
    rows = mask_hbm.at[pl.ds(k0, n_row_k)]
    loads = [
        pltpu.make_async_copy(coeffs_hbm, coeffs, load_sems.at[0]),
        pltpu.make_async_copy(trial_hbm, trial, load_sems.at[1]),
        pltpu.make_async_copy(q_hbm.at[pl.ds(0, 1)], qrow, load_sems.at[2]),
        pltpu.make_async_copy(rows, masks.at[:, pl.ds(0, total)], load_sems.at[3]),
        pltpu.make_async_copy(rows, masks.at[:, pl.ds(total, total)], load_sems.at[4]),
        pltpu.make_async_copy(w_hbm, weights, load_sems.at[5]),
        pltpu.make_async_copy(q_hbm.at[pl.ds(0, 1)], qvec, load_sems.at[6]),
    ]
    for load in loads:
        load.start()
    for load in loads[:2]:
        load.wait()
    own[...] = lax.dot_general(
        trial[0], coeffs[0], (((1,), (1,)), ((), ())), preferred_element_type=jnp.float32
    ).astype(own.dtype)
    started, local = [], []

    def push(src, dst, to):
        k = len(started)
        copy = pltpu.make_async_remote_copy(
            src, dst, send_sems.at[k], recv_sems.at[k], device_id=to, device_id_type=MESH
        )
        copy.start()
        started.append(copy)
        return copy

    def keep(src, dst):
        copy = pltpu.make_async_copy(src, dst, local_sems.at[len(local)])
        copy.start()
        local.append(copy)
        return copy

    def coords(n, steps):
        return {d: None if by is None else moved(at, d, by)[d] for d, by in zip(PARTS[n][3], steps)}

    def region(n, steps):
        where = coords(n, steps)
        return bufs[n].at[tuple(pl.ds(0, SIDE) if where[d] is None else where[d] for d in PARTS[n][4])]

    def place(n, steps):
        where = coords(n, steps)
        h, rows, cols, _, _ = PARTS[n]
        spans = tuple(pl.ds(0, SIDE) if where[d] is None else where[d] for d in "xzy")
        dst = vecs[h].at[spans + (core, pl.ds(rows[0] - 16 * h, rows[1]), pl.ds(*cols))]
        src = region(n, steps)
        return push(src, dst, partner), keep(src, dst)

    def send(n, stage, steps, src=None):
        dim = PARTS[n][3][stage]
        block = region(n, steps)
        return [
            push(block if src is None else src, block, device(moved(at, dim, by), core)) for by in (2, 1, -1)
        ]

    def prepare():
        for load in loads[2:5]:
            load.wait()
        base = col * n_slots
        skip = turn[0] * n_slots

        def scan(j, carry):
            count, picked = carry
            q = qrow[0, j]
            held = (q >= base) & (q < base + n_slots)
            picked = tuple(jnp.where(held & (count == n), j, p) for n, p in enumerate(picked))
            return count + jnp.where(held, 1, 0), picked

        first = (-skip, (jnp.int32(-1),) * n_slots)
        _, picked = lax.fori_loop(0, total, scan, first, unroll=4)
        for n, p in enumerate(picked):
            slots[n] = p
        acc[...] = jnp.zeros_like(acc)
        loads[6].wait()
        first_q = n_slots * lax.broadcasted_iota(jnp.int32, (n_row_k, total), 0)
        held = (qvec[...] >= first_q) & (qvec[...] < first_q + n_slots)
        counts = jnp.sum(jnp.where(held, 1.0, 0.0), axis=1, keepdims=True)
        most[0] = jnp.max(counts).astype(jnp.int32)

    parts = range(len(PARTS))
    mine = [[n for n in parts if PARTS[n][0] == h] for h in range(HALVES)]
    own_piece = [own.at[pl.ds(*PARTS[n][1]), pl.ds(*PARTS[n][2])] for n in parts]
    kept = [keep(own_piece[n], region(n, (0, 0, 0))) for n in parts]
    meet()
    moving = [send(n, 0, (0, 0, 0), own_piece[n]) for n in parts]
    for copy in kept:
        copy.wait()
    for stage, steps in ((1, (None, 0, 0)), (2, (None, None, 0))):
        for n in parts:
            for copy in moving[n]:
                copy.wait_recv()
            moving[n] = send(n, stage, steps)
    placing = [[place(n, (None, None, 0)) for n in mine[h]] for h in range(HALVES)]
    prepare()

    def arrive(h):
        for n in mine[h]:
            for copy, by in zip(moving[n], (2, -1, 1)):
                copy.wait_recv()
                placing[h].append(place(n, (None, None, by)))

    def settle(h):
        for there_copy, here_copy in placing[h]:
            there_copy.wait_recv()
            here_copy.wait()

    nv, rank = own.shape
    part_v = nv // HALVES

    def wrapped(k):
        return jnp.where(k >= total, k - total, k)

    def step(h):
        flat = vecs[h].reshape(total, part_v, rank)

        def side(start, scales):
            blocks = []
            for i in range(n_row_k):
                scale = jnp.full((part_v, rank), scales[i], jnp.float32).astype(own.dtype)
                blocks.append(flat[wrapped(start + i)] * scale)
            return jnp.concatenate(blocks, axis=0)

        def body(n, carry):
            slot = slots[n]
            used = jnp.where(slot >= 0, 1, 0)
            j = jnp.where(slot >= 0, slot, 0)
            w = weights[jnp.where(slot >= 0, qrow[0, j] - col * n_slots, 0)]
            ahead_k = wrapped(k0 + j)
            behind_k = wrapped(k0 + total - j)
            turned_used = jnp.where(slot > 0, 1, 0)
            ahead = [(used * masks[i, ahead_k + i]).astype(jnp.float32) for i in range(n_row_k)]
            behind = [
                (turned_used * (1 - masks[i, behind_k + i])).astype(jnp.float32) for i in range(n_row_k)
            ]
            direct = side(ahead_k, ahead)
            turned = side(behind_k, behind)
            both = lax.dot_general(
                direct, w, (((1,), (1,)), ((), ())), preferred_element_type=jnp.float32
            ) + jnp.dot(turned, w, preferred_element_type=jnp.float32)
            acc[h] += both.reshape(acc.shape[1:])
            return carry

        return body

    def mate(k, c):
        far_z, far_y = there(*spread[k])
        return far_z * 8 + far_y * 2 + c

    def swap(h):
        return [push(acc.at[h, mate(k, 1 - core)], pair.at[h, k], partner) for k in range(8)]

    sends = []

    def collect(h, swaps):
        for k in range(8):
            swaps[k].wait_recv()
            summed = acc[h, mate(k, core)] + pair[h, k]
            if k < 7:
                staged[h, k] = summed.astype(staged.dtype)
            if k > 0:
                sends.append(push(staged.at[h, k - 1], landed.at[h, k - 1], peer(*spread[k - 1])))
        return summed

    def finish(h, summed):
        for k in range(7):
            sends[h * 7 + k].wait_recv()
            summed += landed[h, k].astype(jnp.float32)
        high = summed.astype(jnp.bfloat16)
        low = (summed - high.astype(jnp.float32)).astype(jnp.bfloat16)
        out[0, pl.ds(h * part_v, part_v), :] = jnp.dot(
            high, coeffs[0], preferred_element_type=jnp.float32
        ) + jnp.dot(low, coeffs[0], preferred_element_type=jnp.float32)

    first, second = n_slots * 2 // 8, n_slots * 4 // 8
    arrive(0)
    loads[5].wait()
    settle(0)
    lax.fori_loop(0, first, step(0), 0)
    arrive(1)
    lax.fori_loop(first, n_slots, step(0), 0)
    early = swap(0)
    settle(1)
    lax.fori_loop(0, second, step(1), 0)
    summed0 = collect(0, early)
    lax.fori_loop(second, n_slots, step(1), 0)
    summed1 = collect(1, swap(1))
    finish(0, summed0)
    finish(1, summed1)
    for copy in started:
        copy.wait_send()


def run_round(turn, coeffs, trial, screened, qmap, mask):
    nv, rank, nt = trial.shape[1], coeffs.shape[1], coeffs.shape[2]
    n_slots = screened.shape[0]
    n_row_k = lax.axis_size("col")
    total = qmap.shape[0]
    part_v = nv // HALVES
    local = 5 * len(PARTS)
    remote = 13 * len(PARTS) + 15 * HALVES
    anywhere = pl.BlockSpec(memory_space=pl.ANY)
    return pl.pallas_call(
        lambda *refs: one_round(n_slots, n_row_k, *refs),
        out_shape=(
            jax.ShapeDtypeStruct((1, nv, nt), jnp.float32),
            jax.ShapeDtypeStruct((1,), jnp.int32),
        ),
        in_specs=[pl.BlockSpec(memory_space=pltpu.SMEM)] + [anywhere] * 5,
        out_specs=(pl.BlockSpec(memory_space=pltpu.VMEM), pl.BlockSpec(memory_space=pltpu.SMEM)),
        scratch_shapes=[
            pltpu.VMEM(coeffs.shape, coeffs.dtype),
            pltpu.VMEM(trial.shape, trial.dtype),
            pltpu.VMEM((nv, rank), jnp.bfloat16),
        ]
        + [pltpu.VMEM((SIDE, SIDE, SIDE, part[1][1], part[2][1]), jnp.bfloat16) for part in PARTS]
        + [
            pltpu.VMEM((SIDE, SIDE, SIDE, 2, part_v, rank), jnp.bfloat16) for _ in range(HALVES)
        ]
        + [
            pltpu.VMEM(screened.shape, screened.dtype),
            pltpu.VMEM((HALVES, n_row_k, part_v, rank), jnp.float32),
            pltpu.VMEM((HALVES, 8, part_v, rank), jnp.float32),
            pltpu.VMEM((HALVES, 7, part_v, rank), jnp.bfloat16),
            pltpu.VMEM((HALVES, 7, part_v, rank), jnp.bfloat16),
            pltpu.SMEM((1, total), jnp.int32),
            pltpu.VMEM((1, total), jnp.int32),
            pltpu.SMEM((n_row_k, 2 * total), jnp.int32),
            pltpu.SMEM((n_slots,), jnp.int32),
            pltpu.SemaphoreType.DMA((7,)),
            pltpu.SemaphoreType.DMA((local,)),
            pltpu.SemaphoreType.DMA((remote,)),
            pltpu.SemaphoreType.DMA((remote,)),
        ],
        compiler_params=pltpu.CompilerParams(
            collective_id=0, has_side_effects=True, vmem_limit_bytes=60 * 2**20
        ),
    )(turn, coeffs, trial, screened, qmap, mask)


def per_device(coeffs, trial, screened, qmap, mask):
    n_slots = screened.shape[0]
    args = (coeffs, trial, screened, qmap, mask)
    first, most = run_round(jnp.zeros((1,), jnp.int32), *args)

    def more(state):
        return state[0] * n_slots < most[0]

    def again(state):
        return state[0] + 1, state[1] + run_round(state[0][None], *args)[0]

    return lax.while_loop(more, again, (jnp.int32(1), first))[1]


def solution(mesh):
    return jax.shard_map(
        per_device,
        mesh=mesh,
        in_specs=(
            P(("row", "col"), None, None),
            P(("row", "col"), None, None),
            P("col", None, None),
            P(),
            P(),
        ),
        out_specs=P(("row", "col"), None, None),
        check_vma=False,
    )
```

time: 41.6 us -> 40.4 us (0.971); the launches traced: 40.9 us -> 40.3 us
  Pallas kernels: 39.7 us -> 39 us
    pallas_call x1, Pallas kernels: 39.7 us -> 39 us  [run_round(): pl.pallas_call(lambda *refs: one_round(n_slots, n_row_k, *refs), out_shap...]
where the time goes in v4:
time: 40.4 us; the launch traced here: 40.3 us
  Pallas kernels  39 us (97%)
  local copies, waits for them, and re-layouts  0.62 us (2%)
  loops' own time  0.57 us (1%)
    pallas_call x1, Pallas kernels, run_round(): pl.pallas_call(lambda *refs: one_round(n_slots, n_row_k, *refs), out_shap...  39 us

profile of v4, /device:TPU:0, one launch (start us, length us, event | category | flops | bytes accessed | tf_op | source)
XLA Modules:
  0.0 40.3 jit_solution(14618367677760708183)
XLA Ops:
  0.0 0.0 copy-start.2
  0.0 0.0 copy-start.1
  0.0 0.0 copy-start.3
  0.0 0.0 copy-start
  0.0 39.0 %shard_map.55 = (f32[1,32,128]{2,1,0:T(8,128)S(1)}, s32[1]{0:T(128)}) custom-call(s32[1]{0:T(128)} %constant.4.clone.1.refs_0_, bf16[1,512,128]{2,1,0:T(8,128)(2,1)} %refs_1_.1, bf16[1,32,128]{2,1,0:T(8,128)(2,1)} %refs_2_.1, bf16[8,512,512]{2,1,0:T(8,128)(2,1)} %refs_3_.1, s32[128,128]{1,0:T(8,128)} %refs_4_.1, s32[128,128]{1,0:T(8,128)} %refs_5_.1), custom_call_target="tpu_custom_call" | custom-call | tf_op jit(solution)/shard_map/pallas_call | solution.py:270
  39.0 0.0 copy-done.2
  39.0 0.0 copy-done.1
  39.0 0.0 copy-done.3
  39.1 0.0 copy-done
  39.1 0.6 %while.10 = (s32[]{:T(128)}, f32[1,32,128]{2,1,0:T(8,128)S(1)}, s32[1]{0:T(128)}, bf16[1,512,128]{2,1,0:T(8,128)(2,1)S(1)}, bf16[1,32,128]{2,1,0:T(8,128)(2,1)S(...) while((s32[]{:T(128)}, f32[1,32,128]{2,1,0:T(8,128)S(1)}, ...), condition=%wide.region_1.0_spmd, body=%wide.region_0.0_spmd.sunk | while | flops 4099 | bytes 49265 | solution.py:319
  39.6 0.6 %copy.13 = f32[1,32,128]{2,1,0:T(8,128)} copy(f32[1,32,128]{2,1,0:T(8,128)S(1)} %get-tuple-element.53) | data formatting | bytes 32768
Async XLA Ops:
  0.0 39.0 %copy-start.2 = (s32[128,128]{1,0:T(8,128)S(1)}, s32[128,128]{1,0:T(8,128)}, u32[]{:S(2)}) copy-start(s32[128,128]{1,0:T(8,128)} %refs_5_.1) | copy-start | bytes 196612
  0.0 39.0 %copy-start.1 = (s32[128,128]{1,0:T(8,128)S(1)}, s32[128,128]{1,0:T(8,128)}, u32[]{:S(2)}) copy-start(s32[128,128]{1,0:T(8,128)} %refs_4_.1) | copy-start | bytes 196612
  0.0 39.0 %copy-start.3 = (bf16[1,32,128]{2,1,0:T(8,128)(2,1)S(1)}, bf16[1,32,128]{2,1,0:T(8,128)(2,1)}, u32[]{:S(2)}) copy-start(bf16[1,32,128]{2,1,0:T(8,128)(2,1)} %refs_2_.1) | copy-start | bytes 24580
  0.0 39.1 %copy-start = (bf16[1,512,128]{2,1,0:T(8,128)(2,1)S(1)}, bf16[1,512,128]{2,1,0:T(8,128)(2,1)}, u32[]{:S(2)}) copy-start(bf16[1,512,128]{2,1,0:T(8,128)(2,1)} %refs_1_.1) | copy-start | bytes 393220

commit v5 on v4

--- a/solution.py
+++ b/solution.py
@@ -114,12 +114,10 @@
         src = region(n, steps)
         return push(src, dst, partner), keep(src, dst)
 
-    def send(n, stage, steps, src=None):
+    def send(n, stage, steps, by, src=None):
         dim = PARTS[n][3][stage]
         block = region(n, steps)
-        return [
-            push(block if src is None else src, block, device(moved(at, dim, by), core)) for by in (2, 1, -1)
-        ]
+        return push(block if src is None else src, block, device(moved(at, dim, by), core))
 
     def prepare():
         for load in loads[2:5]:
@@ -150,21 +148,28 @@
     own_piece = [own.at[pl.ds(*PARTS[n][1]), pl.ds(*PARTS[n][2])] for n in parts]
     kept = [keep(own_piece[n], region(n, (0, 0, 0))) for n in parts]
     meet()
-    moving = [send(n, 0, (0, 0, 0), own_piece[n]) for n in parts]
+    moving = [[send(n, 0, (0, 0, 0), by, own_piece[n]) for by in (2, 1, -1)] for n in parts]
     for copy in kept:
         copy.wait()
-    for stage, steps in ((1, (None, 0, 0)), (2, (None, None, 0))):
-        for n in parts:
+    for n in parts:
+        for copy in moving[n]:
+            copy.wait_recv()
+        moving[n] = [send(n, 1, (None, 0, 0), by) for by in (2, 1, -1)]
+    last = []
+    for h in range(HALVES):
+        for n in mine[h]:
             for copy in moving[n]:
                 copy.wait_recv()
-            moving[n] = send(n, stage, steps)
+            last.append([send(n, 2, (None, None, 0), by) for by in (1, -1)])
+        for n in mine[h]:
+            last[n].append(send(n, 2, (None, None, 0), 2))
     placing = [[place(n, (None, None, 0)) for n in mine[h]] for h in range(HALVES)]
     prepare()
 
     def arrive(h):
-        for n in mine[h]:
-            for copy, by in zip(moving[n], (2, -1, 1)):
-                copy.wait_recv()
+        for k, by in enumerate((-1, 1, 2)):
+            for n in mine[h]:
+                last[n][k].wait_recv()
                 placing[h].append(place(n, (None, None, by)))
 
     def settle(h):
@@ -239,7 +244,7 @@
             high, coeffs[0], preferred_element_type=jnp.float32
         ) + jnp.dot(low, coeffs[0], preferred_element_type=jnp.float32)
 
-    first, second = n_slots * 2 // 8, n_slots * 4 // 8
+    first, second = n_slots * 3 // 8, n_slots * 5 // 8
     arrive(0)
     loads[5].wait()
     settle(0)

time: 40.4 us -> 40.1 us (level)
  no operation moved by 1% of the time
where the time goes in v5:
time: 40.1 us; the launch traced here: 39.9 us
  Pallas kernels  38.7 us (97%)
  local copies, waits for them, and re-layouts  0.62 us (2%)
  loops' own time  0.57 us (1%)
    pallas_call x1, Pallas kernels, run_round(): pl.pallas_call(lambda *refs: one_round(n_slots, n_row_k, *refs), out_shap...  38.7 us

profile of v5, /device:TPU:0, one launch (start us, length us, event | category | flops | bytes accessed | tf_op | source)
XLA Modules:
  0.0 39.9 jit_solution(13164062615543527291)
XLA Ops:
  0.0 0.0 copy-start.2
  0.0 0.0 copy-start.1
  0.0 0.0 copy-start.3
  0.0 0.0 copy-start
  0.0 38.7 %shard_map.55 = (f32[1,32,128]{2,1,0:T(8,128)S(1)}, s32[1]{0:T(128)}) custom-call(s32[1]{0:T(128)} %constant.4.clone.1.refs_0_, bf16[1,512,128]{2,1,0:T(8,128)(2,1)} %refs_1_.1, bf16[1,32,128]{2,1,0:T(8,128)(2,1)} %refs_2_.1, bf16[8,512,512]{2,1,0:T(8,128)(2,1)} %refs_3_.1, s32[128,128]{1,0:T(8,128)} %refs_4_.1, s32[128,128]{1,0:T(8,128)} %refs_5_.1), custom_call_target="tpu_custom_call" | custom-call | tf_op jit(solution)/shard_map/pallas_call | solution.py:275
  38.7 0.0 copy-done.2
  38.7 0.0 copy-done.1
  38.7 0.0 copy-done.3
  38.7 0.0 copy-done
  38.7 0.6 %while.10 = (s32[]{:T(128)}, f32[1,32,128]{2,1,0:T(8,128)S(1)}, s32[1]{0:T(128)}, bf16[1,512,128]{2,1,0:T(8,128)(2,1)S(1)}, bf16[1,32,128]{2,1,0:T(8,128)(2,1)S(...) while((s32[]{:T(128)}, f32[1,32,128]{2,1,0:T(8,128)S(1)}, ...), condition=%wide.region_1.0_spmd, body=%wide.region_0.0_spmd.sunk | while | flops 4099 | bytes 49265 | solution.py:324
  39.3 0.6 %copy.13 = f32[1,32,128]{2,1,0:T(8,128)} copy(f32[1,32,128]{2,1,0:T(8,128)S(1)} %get-tuple-element.53) | data formatting | bytes 32768
Async XLA Ops:
  0.0 38.7 %copy-start.2 = (s32[128,128]{1,0:T(8,128)S(1)}, s32[128,128]{1,0:T(8,128)}, u32[]{:S(2)}) copy-start(s32[128,128]{1,0:T(8,128)} %refs_5_.1) | copy-start | bytes 196612
  0.0 38.7 %copy-start.1 = (s32[128,128]{1,0:T(8,128)S(1)}, s32[128,128]{1,0:T(8,128)}, u32[]{:S(2)}) copy-start(s32[128,128]{1,0:T(8,128)} %refs_4_.1) | copy-start | bytes 196612
  0.0 38.7 %copy-start.3 = (bf16[1,32,128]{2,1,0:T(8,128)(2,1)S(1)}, bf16[1,32,128]{2,1,0:T(8,128)(2,1)}, u32[]{:S(2)}) copy-start(bf16[1,32,128]{2,1,0:T(8,128)(2,1)} %refs_2_.1) | copy-start | bytes 24580
  0.0 38.7 %copy-start = (bf16[1,512,128]{2,1,0:T(8,128)(2,1)S(1)}, bf16[1,512,128]{2,1,0:T(8,128)(2,1)}, u32[]{:S(2)}) copy-start(bf16[1,512,128]{2,1,0:T(8,128)(2,1)} %refs_1_.1) | copy-start | bytes 393220

commit v6 on v5

--- a/solution.py
+++ b/solution.py
@@ -9,14 +9,11 @@
 MESH = pl.DeviceIdType.MESH
 SIDE = 4
 HALVES = 2
+ORDERS = (("yzx", "xzy"), ("zxy", "yxz"), ("xyz", "zxy"))
 PARTS = tuple(
-    (h, (16 * h + r, n), cols, order, dims)
+    (h, (16 * h + r, n), cols, *ORDERS[(p + 2 * h) % 3])
     for h in range(HALVES)
-    for r, n, cols, order, dims in (
-        (0, 8, (0, 384), "yzx", "xzy"),
-        (8, 8, (0, 384), "zxy", "yxz"),
-        (0, 16, (384, 128), "xyz", "zxy"),
-    )
+    for p, (r, n, cols) in enumerate(((0, 8, (0, 384)), (8, 8, (0, 384)), (0, 16, (384, 128))))
 )
 
 
@@ -59,10 +56,6 @@
         far_z, far_y = there(a, b)
         return (row, far_z * 8 + far_y * 2 + core)
 
-    meet = greet(
-        [device(moved(at, dim, by), core) for dim in "xyz" for by in (1, -1, 2)]
-        + [partner] + [peer(1, b) for b in (1, 2, 3)]
-    )
     k0 = row * n_row_k
     total = q_hbm.shape[1]
     rows = mask_hbm.at[pl.ds(k0, n_row_k)]
@@ -77,6 +70,10 @@
     ]
     for load in loads:
         load.start()
+    meet = greet(
+        [device(moved(at, dim, by), core) for dim in "xyz" for by in (1, -1, 2)]
+        + [partner] + [peer(1, b) for b in (1, 2, 3)]
+    )
     for load in loads[:2]:
         load.wait()
     own[...] = lax.dot_general(

time: 40.1 us -> 40.1 us (level)
  no operation moved by 1% of the time
where the time goes in v6:
time: 40.1 us; the launch traced here: 39.9 us
  Pallas kernels  38.7 us (97%)
  local copies, waits for them, and re-layouts  0.62 us (2%)
  loops' own time  0.57 us (1%)
    pallas_call x1, Pallas kernels, run_round(): pl.pallas_call(lambda *refs: one_round(n_slots, n_row_k, *refs), out_shap...  38.7 us

profile of v6, /device:TPU:0, one launch (start us, length us, event | category | flops | bytes accessed | tf_op | source)
XLA Modules:
  0.0 39.9 jit_solution(13659543882442864006)
XLA Ops:
  0.0 0.0 copy-start.2
  0.0 0.0 copy-start.1
  0.0 0.0 copy-start.3
  0.0 0.0 copy-start
  0.0 38.7 %shard_map.55 = (f32[1,32,128]{2,1,0:T(8,128)S(1)}, s32[1]{0:T(128)}) custom-call(s32[1]{0:T(128)} %constant.4.clone.1.refs_0_, bf16[1,512,128]{2,1,0:T(8,128)(2,1)} %refs_1_.1, bf16[1,32,128]{2,1,0:T(8,128)(2,1)} %refs_2_.1, bf16[8,512,512]{2,1,0:T(8,128)(2,1)} %refs_3_.1, s32[128,128]{1,0:T(8,128)} %refs_4_.1, s32[128,128]{1,0:T(8,128)} %refs_5_.1), custom_call_target="tpu_custom_call" | custom-call | tf_op jit(solution)/shard_map/pallas_call | solution.py:272
  38.7 0.0 copy-done.2
  38.7 0.0 copy-done.1
  38.7 0.0 copy-done.3
  38.7 0.0 copy-done
  38.7 0.6 %while.10 = (s32[]{:T(128)}, f32[1,32,128]{2,1,0:T(8,128)S(1)}, s32[1]{0:T(128)}, bf16[1,512,128]{2,1,0:T(8,128)(2,1)S(1)}, bf16[1,32,128]{2,1,0:T(8,128)(2,1)S(...) while((s32[]{:T(128)}, f32[1,32,128]{2,1,0:T(8,128)S(1)}, ...), condition=%wide.region_1.0_spmd, body=%wide.region_0.0_spmd.sunk | while | flops 4099 | bytes 49265 | solution.py:321
  39.3 0.6 %copy.13 = f32[1,32,128]{2,1,0:T(8,128)} copy(f32[1,32,128]{2,1,0:T(8,128)S(1)} %get-tuple-element.53) | data formatting | bytes 32768
Async XLA Ops:
  0.0 38.7 %copy-start.2 = (s32[128,128]{1,0:T(8,128)S(1)}, s32[128,128]{1,0:T(8,128)}, u32[]{:S(2)}) copy-start(s32[128,128]{1,0:T(8,128)} %refs_5_.1) | copy-start | bytes 196612
  0.0 38.7 %copy-start.1 = (s32[128,128]{1,0:T(8,128)S(1)}, s32[128,128]{1,0:T(8,128)}, u32[]{:S(2)}) copy-start(s32[128,128]{1,0:T(8,128)} %refs_4_.1) | copy-start | bytes 196612
  0.0 38.7 %copy-start.3 = (bf16[1,32,128]{2,1,0:T(8,128)(2,1)S(1)}, bf16[1,32,128]{2,1,0:T(8,128)(2,1)}, u32[]{:S(2)}) copy-start(bf16[1,32,128]{2,1,0:T(8,128)(2,1)} %refs_2_.1) | copy-start | bytes 24580
  0.0 38.7 %copy-start = (bf16[1,512,128]{2,1,0:T(8,128)(2,1)S(1)}, bf16[1,512,128]{2,1,0:T(8,128)(2,1)}, u32[]{:S(2)}) copy-start(bf16[1,512,128]{2,1,0:T(8,128)(2,1)} %refs_1_.1) | copy-start | bytes 393220

commit v7 on v6

--- a/solution.py
+++ b/solution.py
@@ -241,7 +241,7 @@
             high, coeffs[0], preferred_element_type=jnp.float32
         ) + jnp.dot(low, coeffs[0], preferred_element_type=jnp.float32)
 
-    first, second = n_slots * 3 // 8, n_slots * 5 // 8
+    first, second = n_slots * 3 // 8, n_slots * 4 // 8
     arrive(0)
     loads[5].wait()
     settle(0)

time: 40.1 us -> 40.1 us (level)
  no operation moved by 1% of the time
where the time goes in v7:
time: 40.1 us; the launch traced here: 39.9 us
  Pallas kernels  38.7 us (97%)
  local copies, waits for them, and re-layouts  0.62 us (2%)
  loops' own time  0.57 us (1%)
    pallas_call x1, Pallas kernels, run_round(): pl.pallas_call(lambda *refs: one_round(n_slots, n_row_k, *refs), out_shap...  38.7 us

profile of v7, /device:TPU:0, one launch (start us, length us, event | category | flops | bytes accessed | tf_op | source)
XLA Modules:
  0.0 39.9 jit_solution(1675531606844441185)
XLA Ops:
  0.0 0.0 copy-start.2
  0.0 0.0 copy-start.1
  0.0 0.0 copy-start.3
  0.0 0.0 copy-start
  0.0 38.7 %shard_map.55 = (f32[1,32,128]{2,1,0:T(8,128)S(1)}, s32[1]{0:T(128)}) custom-call(s32[1]{0:T(128)} %constant.4.clone.1.refs_0_, bf16[1,512,128]{2,1,0:T(8,128)(2,1)} %refs_1_.1, bf16[1,32,128]{2,1,0:T(8,128)(2,1)} %refs_2_.1, bf16[8,512,512]{2,1,0:T(8,128)(2,1)} %refs_3_.1, s32[128,128]{1,0:T(8,128)} %refs_4_.1, s32[128,128]{1,0:T(8,128)} %refs_5_.1), custom_call_target="tpu_custom_call" | custom-call | tf_op jit(solution)/shard_map/pallas_call | solution.py:272
  38.7 0.0 copy-done.2
  38.7 0.0 copy-done.1
  38.7 0.0 copy-done.3
  38.7 0.0 copy-done
  38.7 0.6 %while.10 = (s32[]{:T(128)}, f32[1,32,128]{2,1,0:T(8,128)S(1)}, s32[1]{0:T(128)}, bf16[1,512,128]{2,1,0:T(8,128)(2,1)S(1)}, bf16[1,32,128]{2,1,0:T(8,128)(2,1)S(...) while((s32[]{:T(128)}, f32[1,32,128]{2,1,0:T(8,128)S(1)}, ...), condition=%wide.region_1.0_spmd, body=%wide.region_0.0_spmd.sunk | while | flops 4099 | bytes 49265 | solution.py:321
  39.3 0.6 %copy.13 = f32[1,32,128]{2,1,0:T(8,128)} copy(f32[1,32,128]{2,1,0:T(8,128)S(1)} %get-tuple-element.53) | data formatting | bytes 32768
Async XLA Ops:
  0.0 38.7 %copy-start.2 = (s32[128,128]{1,0:T(8,128)S(1)}, s32[128,128]{1,0:T(8,128)}, u32[]{:S(2)}) copy-start(s32[128,128]{1,0:T(8,128)} %refs_5_.1) | copy-start | bytes 196612
  0.0 38.7 %copy-start.1 = (s32[128,128]{1,0:T(8,128)S(1)}, s32[128,128]{1,0:T(8,128)}, u32[]{:S(2)}) copy-start(s32[128,128]{1,0:T(8,128)} %refs_4_.1) | copy-start | bytes 196612
  0.0 38.7 %copy-start.3 = (bf16[1,32,128]{2,1,0:T(8,128)(2,1)S(1)}, bf16[1,32,128]{2,1,0:T(8,128)(2,1)}, u32[]{:S(2)}) copy-start(bf16[1,32,128]{2,1,0:T(8,128)(2,1)} %refs_2_.1) | copy-start | bytes 24580
  0.0 38.7 %copy-start = (bf16[1,512,128]{2,1,0:T(8,128)(2,1)S(1)}, bf16[1,512,128]{2,1,0:T(8,128)(2,1)}, u32[]{:S(2)}) copy-start(bf16[1,512,128]{2,1,0:T(8,128)(2,1)} %refs_1_.1) | copy-start | bytes 393220
